TPU v7x, 32 devices: a whole 2x2x4 slice. The times are simulated.
32 devices in a mesh: clip: 8 (over y, x, core), frame: 4 (over z).
Axes of the slice: x: 2, y: 2, z: 4, core: 2. Of those that a mesh axis runs over, the one named last changes fastest.
Arguments:
- big_tokens: bfloat16 [8, 16, 256, 1024], P('clip', 'frame'), may hold values from -6 to 6
- small_tokens: bfloat16 [8, 16, 64, 1024], P('clip', 'frame'), may hold values from -6 to 6
- big_actions: int32 [8, 16], P('clip', 'frame'), may hold values from 0 to 7
- small_actions: int32 [8, 16], P('clip', 'frame'), may hold values from 0 to 7
- action_table: bfloat16 [8, 1024], P(None, ('clip', 'frame')), may hold values from -3 to 3
- norm_gain: bfloat16 [3, 1024], P(None, ('clip', 'frame')), may hold values from 0.099609375 to 1.8984375
- norm_bias: bfloat16 [3, 1024], P(None, ('clip', 'frame')), may hold values from -3 to 3
- spatial_inputs: bfloat16 [1024, 3072], P('frame', 'clip'), may hold values from -0.1875 to 0.1875
- spatial_output: bfloat16 [1024, 1024], P('frame', 'clip'), may hold values from -2 to 2
- temporal_inputs: bfloat16 [1024, 3072], P('frame', 'clip'), may hold values from -0.1875 to 0.1875
- temporal_output: bfloat16 [1024, 1024], P('frame', 'clip'), may hold values from -0.5 to 0.5
- up_weight: bfloat16 [1024, 4096], P('frame', 'clip'), may hold values from -0.1875 to 0.1875
- down_weight: bfloat16 [4096, 1024], P('frame', 'clip'), may hold values from -0.09375 to 0.09375
- branch_bias: bfloat16 [3, 1024], P(None, ('clip', 'frame')), may hold values from -2 to 2
- hidden_bias: bfloat16 [4096], P(('clip', 'frame')), may hold values from -3 to 3
- big_cotangent: bfloat16 [8, 16, 256, 1024], P('clip', 'frame'), may hold values from -6 to 6
- small_cotangent: bfloat16 [8, 16, 64, 1024], P('clip', 'frame'), may hold values from -6 to 6
Outputs:
- big_output: bfloat16 [8, 16, 256, 1024], P('clip', 'frame')
- small_output: bfloat16 [8, 16, 64, 1024], P('clip', 'frame')
- big_gradient: float32 [8, 16, 256, 1024], P('clip', 'frame')
- small_gradient: float32 [8, 16, 64, 1024], P('clip', 'frame')
- table_gradient: float32 [8, 1024], P(None, ('clip', 'frame'))
- gain_gradient: float32 [3, 1024], P(None, ('clip', 'frame'))
- bias_gradient: float32 [3, 1024], P(None, ('clip', 'frame'))
- spatial_inputs_gradient: float32 [1024, 3072], P('frame', 'clip')
- spatial_output_gradient: float32 [1024, 1024], P('frame', 'clip')
- temporal_inputs_gradient: float32 [1024, 3072], P('frame', 'clip')
- temporal_output_gradient: float32 [1024, 1024], P('frame', 'clip')
- up_gradient: float32 [1024, 4096], P('frame', 'clip')
- down_gradient: float32 [4096, 1024], P('frame', 'clip')
- branch_bias_gradient: float32 [3, 1024], P(None, ('clip', 'frame'))
- hidden_bias_gradient: float32 [4096], P(('clip', 'frame'))
All inputs are finite; a program needn't handle non-finite values.
Results may differ from a plain program's by a relative error of at most 0.019.
Values may be sent and summed in bfloat16 or wider, within the bound.
No kernel may reach another device: no remote copies, remote signals or barrier semaphores. Data moves between devices by JAX's collectives and lax.ppermute only.
A program may use at most 320 MiB of HBM per device.

v0:
```python
from functools import partial

import jax
import jax.numpy as jnp
from jax import lax
from jax.sharding import PartitionSpec as P

HEAD_DIM = 64


EPSILON = 1e-05
SCORE_SCALE = 0.125
MASK_FILL = -1e30
HIGHEST = lax.Precision.HIGHEST


def layer_norm(values, norm_gain, offset):
    center = values - jnp.mean(values, axis=-1, keepdims=True)
    spread = jnp.mean(center * center, axis=-1, keepdims=True)
    return center * lax.rsqrt(spread + EPSILON) * norm_gain + offset


def project(activation, weight):
    return jnp.dot(activation, weight, preferred_element_type=jnp.float32)


def outer_sum(left_side, right_side):
    flat_left = left_side.reshape(-1, left_side.shape[-1])
    flat_right = right_side.reshape(-1, right_side.shape[-1])
    return lax.dot_general(
        flat_left, flat_right, (((0,), (0,)), ((), ())), preferred_element_type=jnp.float32
    )


def through(gradient, weight):
    return lax.dot_general(
        gradient,
        weight,
        (((gradient.ndim - 1,), (1,)), ((), ())),
        preferred_element_type=jnp.float32,
    )


def combine_sets(earlier, later):
    return tuple((one_part + other_part for one_part, other_part in zip(earlier, later)))


def masked(scores, causal):
    if causal:
        length = scores.shape[-1]
        rows_index = lax.broadcasted_iota(jnp.int32, (length, length), 0)
        cols_index = lax.broadcasted_iota(jnp.int32, (length, length), 1)
        return jnp.where(rows_index >= cols_index, scores, MASK_FILL)
    return scores


def to_sequences(tensor, causal):
    if causal:
        tensor = jnp.swapaxes(tensor, 1, 2)
    return tensor.reshape((-1,) + tensor.shape[2:])


def from_sequences(tensor, leading, causal):
    if causal:
        return jnp.swapaxes(tensor.reshape((leading[0], leading[2], leading[1], -1)), 1, 2)
    return tensor.reshape(leading + (-1,))


def split_heads(packed, causal):
    head_count = packed.shape[-1] // (3 * HEAD_DIM)
    pieces = packed.reshape(packed.shape[:-1] + (3, head_count, HEAD_DIM))
    return tuple((to_sequences(pieces[..., member, :, :], causal) for member in range(3)))


def score_rows(query_rows, key_rows, causal):
    raw_scores = jnp.einsum(
        "bqhd,bkhd->bhqk", query_rows, key_rows, preferred_element_type=jnp.float32
    )
    return masked(raw_scores * SCORE_SCALE, causal)


def attend(query_rows, key_rows, value_rows, causal):
    scores = score_rows(query_rows, key_rows, causal)
    row_top = jnp.max(scores, axis=-1, keepdims=True)
    exponent = jnp.exp(scores - row_top)
    row_total = jnp.sum(exponent, axis=-1, keepdims=True)
    weights = (exponent / row_total).astype(jnp.bfloat16)
    mixture = jnp.einsum("bhqk,bkhd->bqhd", weights, value_rows, preferred_element_type=jnp.float32)
    return (mixture, row_top, row_total)


def attend_back(query_rows, key_rows, value_rows, row_top, row_total, grad_heads, causal):
    scores = score_rows(query_rows, key_rows, causal)
    probs = jnp.exp(scores - row_top) / row_total
    rounded = probs.astype(jnp.bfloat16)
    grad_value = jnp.einsum(
        "bhqk,bqhd->bkhd", rounded, grad_heads, preferred_element_type=jnp.float32
    )
    grad_probs = jnp.einsum(
        "bqhd,bkhd->bhqk", grad_heads, value_rows, preferred_element_type=jnp.float32
    )
    inner = jnp.sum(probs * grad_probs, axis=-1, keepdims=True)
    grad_scores = (probs * (grad_probs - inner)).astype(jnp.bfloat16)
    grad_query = (
        jnp.einsum("bhqk,bkhd->bqhd", grad_scores, key_rows, preferred_element_type=jnp.float32)
        * SCORE_SCALE
    )
    grad_key = (
        jnp.einsum("bhqk,bqhd->bkhd", grad_scores, query_rows, preferred_element_type=jnp.float32)
        * SCORE_SCALE
    )
    return (grad_query, grad_key, grad_value)


def mix_forward(start, norm_gain, offset, weight_inputs, weight_out, bias_out, causal):
    normed = layer_norm(start, norm_gain, offset).astype(jnp.bfloat16)
    packed = project(normed, weight_inputs).astype(jnp.bfloat16)
    query_rows, key_rows, value_rows = split_heads(packed, causal)
    attended, row_top, row_total = attend(query_rows, key_rows, value_rows, causal)
    mixture = from_sequences(attended, start.shape[:3], causal).astype(jnp.bfloat16)
    result = start + (project(mixture, weight_out) + bias_out)
    return (result.astype(jnp.bfloat16), (normed, packed, row_top, row_total, mixture))


def mix_backward(incoming, start, stored, norm_gain, offset, weight_inputs, weight_out, causal):
    normed, packed, row_top, row_total, mixture = stored
    leading = start.shape[:3]
    grad_out_weight = outer_sum(mixture, incoming)
    grad_out_bias = jnp.sum(incoming.astype(jnp.float32), axis=(0, 1, 2))
    grad_mixture = through(incoming, weight_out).astype(jnp.bfloat16)
    head_count = grad_mixture.shape[-1] // HEAD_DIM
    grad_heads = to_sequences(grad_mixture.reshape(leading + (head_count, HEAD_DIM)), causal)
    query_rows, key_rows, value_rows = split_heads(packed, causal)
    grad_parts = attend_back(
        query_rows, key_rows, value_rows, row_top, row_total, grad_heads, causal
    )
    grad_packed = jnp.concatenate(
        [from_sequences(part_grad, leading, causal) for part_grad in grad_parts], axis=-1
    ).astype(jnp.bfloat16)
    grad_in_weight = outer_sum(normed, grad_packed)
    grad_normed = through(grad_packed, weight_inputs)
    norm_pull = jax.vjp(layer_norm, start, norm_gain, offset)[1]
    grad_start, grad_gain, grad_offset = norm_pull(grad_normed)
    return (
        incoming.astype(jnp.float32) + grad_start,
        (grad_gain, grad_offset, grad_in_weight, grad_out_weight, grad_out_bias),
    )


def ffn_forward(start, norm_gain, offset, weight_up, bias_up, weight_down, bias_down):
    normed = layer_norm(start, norm_gain, offset).astype(jnp.bfloat16)
    hidden = project(normed, weight_up) + bias_up
    active = jax.nn.gelu(hidden, approximate=True).astype(jnp.bfloat16)
    result = start + (project(active, weight_down) + bias_down)
    return (result.astype(jnp.bfloat16), (normed, hidden, active))


def ffn_backward(cotangent, start, stored, norm_gain, offset, weight_up, weight_down):
    normed, hidden, active = stored
    grad_down = outer_sum(active, cotangent)
    grad_bias_down = jnp.sum(cotangent.astype(jnp.float32), axis=(0, 1, 2))
    grad_active = through(cotangent, weight_down)
    gelu_pull = jax.vjp(partial(jax.nn.gelu, approximate=True), hidden)[1]
    grad_hidden = gelu_pull(grad_active)[0].astype(jnp.bfloat16)
    grad_up = outer_sum(normed, grad_hidden)
    grad_bias_up = jnp.sum(grad_hidden.astype(jnp.float32), axis=(0, 1, 2))
    grad_normed = through(grad_hidden, weight_up)
    norm_pull = jax.vjp(layer_norm, start, norm_gain, offset)[1]
    grad_start, grad_gain, grad_offset = norm_pull(grad_normed)
    total_grad = (cotangent.astype(jnp.float32) + grad_start).astype(jnp.bfloat16)
    return (total_grad, (grad_gain, grad_offset, grad_up, grad_down, grad_bias_up, grad_bias_down))


def body(
    big_tokens,
    small_tokens,
    big_actions,
    small_actions,
    action_table,
    norm_gain,
    norm_bias,
    spatial_inputs,
    spatial_output,
    temporal_inputs,
    temporal_output,
    up_weight,
    down_weight,
    branch_bias,
    hidden_bias,
    big_cotangent,
    small_cotangent,
):
    (
        row_table,
        row_gain,
        row_bias,
        row_si,
        row_so,
        row_ti,
        row_to,
        row_up,
        row_down,
        row_branch,
        row_hidden,
    ) = (
        lax.all_gather(action_table, "frame", axis=1, tiled=True),
        lax.all_gather(norm_gain, "frame", axis=1, tiled=True),
        lax.all_gather(norm_bias, "frame", axis=1, tiled=True),
        lax.all_gather(spatial_inputs, "frame", axis=0, tiled=True),
        lax.all_gather(spatial_output, "frame", axis=0, tiled=True),
        lax.all_gather(temporal_inputs, "frame", axis=0, tiled=True),
        lax.all_gather(temporal_output, "frame", axis=0, tiled=True),
        lax.all_gather(up_weight, "frame", axis=0, tiled=True),
        lax.all_gather(down_weight, "frame", axis=0, tiled=True),
        lax.all_gather(branch_bias, "frame", axis=1, tiled=True),
        lax.all_gather(hidden_bias, "frame", axis=0, tiled=True),
    )
    (
        whole_table,
        whole_gain,
        whole_bias,
        whole_spatial_inputs,
        whole_spatial_output,
        whole_temporal_inputs,
        whole_temporal_output,
        whole_up,
        whole_down,
        whole_branch,
        whole_hidden,
    ) = (
        lax.all_gather(row_table, "clip", axis=1, tiled=True),
        lax.all_gather(row_gain, "clip", axis=1, tiled=True),
        lax.all_gather(row_bias, "clip", axis=1, tiled=True),
        lax.all_gather(row_si, "clip", axis=1, tiled=True),
        lax.all_gather(row_so, "clip", axis=1, tiled=True),
        lax.all_gather(row_ti, "clip", axis=1, tiled=True),
        lax.all_gather(row_to, "clip", axis=1, tiled=True),
        lax.all_gather(row_up, "clip", axis=1, tiled=True),
        lax.all_gather(row_down, "clip", axis=1, tiled=True),
        lax.all_gather(row_branch, "clip", axis=1, tiled=True),
        lax.all_gather(row_hidden, "clip", axis=0, tiled=True),
    )
    table_values = whole_table.astype(jnp.float32)
    gain_values = whole_gain.astype(jnp.float32)
    bias_values = whole_bias.astype(jnp.float32)
    branch_values = whole_branch.astype(jnp.float32)
    sub_batches = ((big_tokens, big_actions), (small_tokens, small_actions))
    cotangents = (big_cotangent, small_cotangent)
    onehot_list = []
    start_list = []
    spatial_sent = []
    spatial_stored = []
    for tokens, action_ids in sub_batches:
        onehot_rows = (
            action_ids[..., None] == jnp.arange(table_values.shape[0], dtype=jnp.int32)
        ).astype(jnp.float32)
        embedded = jnp.dot(
            onehot_rows, table_values, precision=HIGHEST, preferred_element_type=jnp.float32
        )
        start = tokens.astype(jnp.float32) + embedded[:, :, None, :]
        sent_rows, stored = mix_forward(
            start,
            gain_values[0],
            bias_values[0],
            whole_spatial_inputs,
            whole_spatial_output,
            branch_values[0],
            False,
        )
        onehot_list.append(onehot_rows)
        start_list.append(start)
        spatial_sent.append(sent_rows)
        spatial_stored.append(stored)
    by_position = (
        lax.all_to_all(spatial_sent[0], "frame", split_axis=2, concat_axis=1, tiled=True),
        lax.all_to_all(spatial_sent[1], "frame", split_axis=2, concat_axis=1, tiled=True),
    )
    residual_list = []
    temporal_sent = []
    temporal_stored = []
    for arriving in by_position:
        residual = arriving.astype(jnp.float32)
        sent_rows, stored = mix_forward(
            residual,
            gain_values[1],
            bias_values[1],
            whole_temporal_inputs,
            whole_temporal_output,
            branch_values[1],
            True,
        )
        residual_list.append(residual)
        temporal_sent.append(sent_rows)
        temporal_stored.append(stored)
    by_frame = (
        lax.all_to_all(temporal_sent[0], "frame", split_axis=1, concat_axis=2, tiled=True),
        lax.all_to_all(temporal_sent[1], "frame", split_axis=1, concat_axis=2, tiled=True),
    )
    hidden_values = whole_hidden.astype(jnp.float32)
    outputs = []
    back_sent = []
    ffn_total = None
    for member in range(2):
        start = by_frame[member].astype(jnp.float32)
        result, stored = ffn_forward(
            start,
            gain_values[2],
            bias_values[2],
            whole_up,
            hidden_values,
            whole_down,
            branch_values[2],
        )
        outputs.append(result)
        grad_sent, gradients = ffn_backward(
            cotangents[member], start, stored, gain_values[2], bias_values[2], whole_up, whole_down
        )
        back_sent.append(grad_sent)
        ffn_total = gradients if ffn_total is None else combine_sets(ffn_total, gradients)
    ffn_gain, ffn_offset, grad_up, grad_down, grad_hidden_bias, grad_down_bias = ffn_total
    back_position = (
        lax.all_to_all(back_sent[0], "frame", split_axis=2, concat_axis=1, tiled=True),
        lax.all_to_all(back_sent[1], "frame", split_axis=2, concat_axis=1, tiled=True),
    )
    temporal_back = []
    temporal_total = None
    for member in range(2):
        grad_start, gradients = mix_backward(
            back_position[member],
            residual_list[member],
            temporal_stored[member],
            gain_values[1],
            bias_values[1],
            whole_temporal_inputs,
            whole_temporal_output,
            True,
        )
        temporal_back.append(grad_start.astype(jnp.bfloat16))
        temporal_total = (
            gradients if temporal_total is None else combine_sets(temporal_total, gradients)
        )
    back_frame = (
        lax.all_to_all(temporal_back[0], "frame", split_axis=1, concat_axis=2, tiled=True),
        lax.all_to_all(temporal_back[1], "frame", split_axis=1, concat_axis=2, tiled=True),
    )
    input_grads = []
    spatial_total = None
    table_total = None
    for member in range(2):
        grad_start, gradients = mix_backward(
            back_frame[member],
            start_list[member],
            spatial_stored[member],
            gain_values[0],
            bias_values[0],
            whole_spatial_inputs,
            whole_spatial_output,
            False,
        )
        input_grads.append(grad_start)
        spatial_total = (
            gradients if spatial_total is None else combine_sets(spatial_total, gradients)
        )
        frame_sums = jnp.sum(grad_start, axis=2)
        table_part = jnp.einsum(
            "cfa,cfd->ad",
            onehot_list[member],
            frame_sums,
            precision=HIGHEST,
            preferred_element_type=jnp.float32,
        )
        table_total = table_part if table_total is None else table_total + table_part
    gain_stack = jnp.stack([spatial_total[0], temporal_total[0], ffn_gain])
    bias_stack = jnp.stack([spatial_total[1], temporal_total[1], ffn_offset])
    branch_stack = jnp.stack([spatial_total[4], temporal_total[4], grad_down_bias])
    (
        column_table,
        column_gain,
        column_bias,
        column_si,
        column_so,
        column_ti,
        column_to,
        column_up,
        column_down,
        column_branch,
        column_hidden,
    ) = (
        lax.psum_scatter(
            table_total.astype(jnp.bfloat16), "clip", scatter_dimension=1, tiled=True
        ).astype(jnp.float32),
        lax.psum_scatter(
            gain_stack.astype(jnp.bfloat16), "clip", scatter_dimension=1, tiled=True
        ).astype(jnp.float32),
        lax.psum_scatter(
            bias_stack.astype(jnp.bfloat16), "clip", scatter_dimension=1, tiled=True
        ).astype(jnp.float32),
        lax.psum_scatter(
            spatial_total[2].astype(jnp.bfloat16), "clip", scatter_dimension=1, tiled=True
        ).astype(jnp.float32),
        lax.psum_scatter(
            spatial_total[3].astype(jnp.bfloat16), "clip", scatter_dimension=1, tiled=True
        ).astype(jnp.float32),
        lax.psum_scatter(
            temporal_total[2].astype(jnp.bfloat16), "clip", scatter_dimension=1, tiled=True
        ).astype(jnp.float32),
        lax.psum_scatter(
            temporal_total[3].astype(jnp.bfloat16), "clip", scatter_dimension=1, tiled=True
        ).astype(jnp.float32),
        lax.psum_scatter(
            grad_up.astype(jnp.bfloat16), "clip", scatter_dimension=1, tiled=True
        ).astype(jnp.float32),
        lax.psum_scatter(
            grad_down.astype(jnp.bfloat16), "clip", scatter_dimension=1, tiled=True
        ).astype(jnp.float32),
        lax.psum_scatter(
            branch_stack.astype(jnp.bfloat16), "clip", scatter_dimension=1, tiled=True
        ).astype(jnp.float32),
        lax.psum_scatter(
            grad_hidden_bias.astype(jnp.bfloat16), "clip", scatter_dimension=0, tiled=True
        ).astype(jnp.float32),
    )
    (
        table_gradient,
        gain_gradient,
        bias_gradient,
        spatial_inputs_gradient,
        spatial_output_gradient,
        temporal_inputs_gradient,
        temporal_output_gradient,
        up_gradient,
        down_gradient,
        branch_bias_gradient,
        hidden_bias_gradient,
    ) = (
        lax.psum_scatter(
            column_table.astype(jnp.bfloat16), "frame", scatter_dimension=1, tiled=True
        ).astype(jnp.float32),
        lax.psum_scatter(
            column_gain.astype(jnp.bfloat16), "frame", scatter_dimension=1, tiled=True
        ).astype(jnp.float32),
        lax.psum_scatter(
            column_bias.astype(jnp.bfloat16), "frame", scatter_dimension=1, tiled=True
        ).astype(jnp.float32),
        lax.psum_scatter(
            column_si.astype(jnp.bfloat16), "frame", scatter_dimension=0, tiled=True
        ).astype(jnp.float32),
        lax.psum_scatter(
            column_so.astype(jnp.bfloat16), "frame", scatter_dimension=0, tiled=True
        ).astype(jnp.float32),
        lax.psum_scatter(
            column_ti.astype(jnp.bfloat16), "frame", scatter_dimension=0, tiled=True
        ).astype(jnp.float32),
        lax.psum_scatter(
            column_to.astype(jnp.bfloat16), "frame", scatter_dimension=0, tiled=True
        ).astype(jnp.float32),
        lax.psum_scatter(
            column_up.astype(jnp.bfloat16), "frame", scatter_dimension=0, tiled=True
        ).astype(jnp.float32),
        lax.psum_scatter(
            column_down.astype(jnp.bfloat16), "frame", scatter_dimension=0, tiled=True
        ).astype(jnp.float32),
        lax.psum_scatter(
            column_branch.astype(jnp.bfloat16), "frame", scatter_dimension=1, tiled=True
        ).astype(jnp.float32),
        lax.psum_scatter(
            column_hidden.astype(jnp.bfloat16), "frame", scatter_dimension=0, tiled=True
        ).astype(jnp.float32),
    )
    return (
        outputs[0],
        outputs[1],
        input_grads[0],
        input_grads[1],
        table_gradient,
        gain_gradient,
        bias_gradient,
        spatial_inputs_gradient,
        spatial_output_gradient,
        temporal_inputs_gradient,
        temporal_output_gradient,
        up_gradient,
        down_gradient,
        branch_bias_gradient,
        hidden_bias_gradient,
    )


def solution(mesh):
    placed = (
        P("clip", "frame", None, None),
        P("clip", "frame", None, None),
        P("clip", "frame"),
        P("clip", "frame"),
        P(None, ("clip", "frame")),
        P(None, ("clip", "frame")),
        P(None, ("clip", "frame")),
        P("frame", "clip"),
        P("frame", "clip"),
        P("frame", "clip"),
        P("frame", "clip"),
        P("frame", "clip"),
        P("frame", "clip"),
        P(None, ("clip", "frame")),
        P(("clip", "frame")),
        P("clip", "frame", None, None),
        P("clip", "frame", None, None),
    )
    return jax.shard_map(
        body,
        mesh=mesh,
        in_specs=placed,
        out_specs=(
            P("clip", "frame", None, None),
            P("clip", "frame", None, None),
            P("clip", "frame", None, None),
            P("clip", "frame", None, None),
            P(None, ("clip", "frame")),
            P(None, ("clip", "frame")),
            P(None, ("clip", "frame")),
            P("frame", "clip"),
            P("frame", "clip"),
            P("frame", "clip"),
            P("frame", "clip"),
            P("frame", "clip"),
            P("frame", "clip"),
            P(None, ("clip", "frame")),
            P(("clip", "frame")),
        ),
        check_vma=False,
    )
```

profile of v0, /device:TPU:0, one launch (start us, length us, event | category | flops | bytes accessed | tf_op | source)
XLA Modules:
  0.0 1639.9 jit_solution(9059308813033123085)
XLA Ops:
  8.8 27.0 %all_gather.72 = bf16[1024,384]{1,0:T(8,128)(2,1)} all-gather(bf16[256,384]{1,0:T(8,128)(2,1)} %param.24), channel_id=1, replica_groups=mesh['clip'=8,'frame'=4] {'frame'}, dimensions={0}, use_global_device_ids=true | all-gather | bytes 983040 | tf_op jit(solution)/shard_map/all_gather | solution.py:209
  35.9 18.1 %all_gather.74 = bf16[1024,128]{1,0:T(8,128)(2,1)} all-gather(bf16[256,128]{1,0:T(8,128)(2,1)} %param.25), channel_id=1, replica_groups=mesh['clip'=8,'frame'=4] {'frame'}, dimensions={0}, use_global_device_ids=true | all-gather | bytes 327680 | tf_op jit(solution)/shard_map/all_gather | solution.py:210
  54.1 26.5 %all_gather.78 = bf16[1024,384]{1,0:T(8,128)(2,1)} all-gather(bf16[256,384]{1,0:T(8,128)(2,1)} %param.26), channel_id=1, replica_groups=mesh['clip'=8,'frame'=4] {'frame'}, dimensions={0}, use_global_device_ids=true | all-gather | bytes 983040 | tf_op jit(solution)/shard_map/all_gather | solution.py:211
  80.7 16.0 all_gather.80
  97.6 11.9 all-gather
  206.7 11.6 fusion.54
  227.0 10.5 fusion.154
  237.5 19.4 %fusion.304 = (f32[4,16,256]{2,1,0:T(8,128)S(1)}, f32[4,16,256,256]{2,3,1,0:T(8,128)}) fusion(f32[4,16,256,256]{2,3,1,0:T(8,128)} %fusion.154), kind=kOutput, calls=%fused_computation.393 | output fusion | flops 16777472 | bytes 33619968 | tf_op jit(solution)/shard_map/sub | solution.py:85
  317.3 39.5 %all-gather.4 = bf16[4,1,128]{2,1,0:T(2,128)(2,1)S(1)} all-gather(bf16[1,1,128]{2,1,0:T(2,128)(2,1)S(1)} %bitcast.855), channel_id=1, replica_groups=mesh['clip'=8,'frame'=4] {'frame'}, dimensions={0}, use_global_device_ids=true | all-gather | bytes 1280 | tf_op jit(solution)/shard_map/all_gather | solution.py:216
  387.1 16.0 reshape.1380
  420.7 12.6 fusion.305
  441.5 12.5 convert_reduce_fusion.2
  458.7 13.5 all-to-all-start.6
  535.7 13.2 all-to-all-done.1
  561.4 16.3 fusion.32
  577.7 24.6 %convert_reduce_fusion = (f32[4096]{0:T(1024)}, bf16[4,256,4096]{2,1,0:T(8,128)(2,1)}) fusion(f32[4,256,4096]{2,1,0:T(8,128)} %fusion.32, f32[4096]{0:T(1024)S(1)} %bitcast.825, bf16[4096,1024]{1,0:T(8,128)(2,1)} %all-gather.29.cloned.1.call-done, bf16[1,4,256,1024]{3,2,1,0:T(8,128)(2,1)S(1)} %copy-done.52), kind=kOutput, calls=%fused_computation.17 | convolution fusion | flops 8686399488 | bytes 35684352 | tf_op jit(solution)/shard_map/dot_general | solution.py:36
  602.3 15.1 fusion.293
  653.6 23.0 %all-to-all-done.4 = bf16[1,4,256,1024]{3,1,0,2:T(4,128)(2,1)S(1)} async-done(((bf16[1,4,256,1024]{3,1,0,2:T(4,128)(2,1)}), bf16[1,4,256,1024]{3,1,0,2:T(4,128)(2,1)S(1)}, u32[]{:S(2)}, u32[]{:S(2)}) %all-to-all-start.4) | async-done | bytes 2097184 | tf_op jit(solution)/shard_map/all_to_all | solution.py:322
  689.1 15.3 multiply_reduce_fusion.2
  763.2 11.7 fusion.292
  803.3 29.9 %all-to-all-done.5 = bf16[1,16,64,1024]{3,2,0,1:T(8,128)(2,1)} async-done(((bf16[1,16,64,1024]{3,2,0,1:T(8,128)(2,1)}), bf16[1,16,64,1024]{3,2,0,1:T(8,128)(2,1)}, u32[]{:S(2)}, u32[]{:S(2)}) %all-to-all-start.5) | async-done | bytes 2097184 | tf_op jit(solution)/shard_map/all_to_all | solution.py:343
  849.2 12.9 multiply_reduce_fusion
  862.0 11.7 multiply_convert_fusion
  880.7 10.0 fusion.148
  902.5 12.3 fusion.74
  950.8 11.3 fusion.108
  977.9 15.0 fusion.310
  992.9 11.5 fusion.12
  1006.1 19.7 %fusion.113 = f32[4096,1024,1]{1,0,2:T(8,128)} fusion(bf16[1,4,256,1024]{3,2,1,0:T(8,128)(2,1)S(1)} %copy-done.53, f32[4,256,4096]{2,1,0:T(8,128)} %fusion.32, f32[4096]{0:T(1024)S(1)} %bitcast.826), kind=kOutput, calls=%fused_computation.160 | convolution fusion | flops 8631877632 | bytes 35667968 | tf_op jit(solution)/shard_map/dot_general | solution.py:30
  1035.4 11.8 copy.488
  1056.3 16.6 %fusion.17 = bf16[1024,3072]{1,0:T(8,128)(2,1)} fusion(f32[1024,3072,1]{1,0,2:T(8,128)} %fusion.245, bf16[4,256,1024]{2,1,0:T(8,128)(2,1)} %copy.406, bf16[4,256,1024]{2,1,0:T(8,128)(2,1)} %copy.405, bf16[4,256,1024]{2,1,0:T(8,128)(2,1)} %copy.404, bf16[1,4,256,1024]{3,2,1,0:T(8,128)(2,1)S(1)} %copy-done.13, f32[1024]{0:T(1024)S(1)} %bitcast.842, ...), kind=kOutput, calls=%fused_computation.27 | convolution fusion | flops 6474956800 | bytes 27295744 | tf_op jit(solution)/shard_map/dot_general | solution.py:30
  1086.4 38.1 %reduce-scatter.75.cloned.1.call-done = bf16[128,1024]{1,0:T(8,128)(2,1)} async-done(((bf16[1024,1024]{1,0:T(8,128)(2,1)}), bf16[128,1024]{1,0:T(8,128)(2,1)}) %reduce-scatter.75.cloned.1.call-update) | async-done | bytes 262160
  1126.4 63.1 %reduce-scatter.77.cloned.1.call-done = bf16[384,1024]{1,0:T(8,128)(2,1)} async-done(((bf16[3072,1024]{1,0:T(8,128)(2,1)}), bf16[384,1024]{1,0:T(8,128)(2,1)}) %reduce-scatter.77.cloned.1.call-update) | async-done | bytes 786448
  1191.9 72.3 %reduce-scatter.55.cloned.1.call-done = bf16[1024,512]{1,0:T(8,128)(2,1)} async-done(((bf16[1024,4096]{1,0:T(8,128)(2,1)}), bf16[1024,512]{1,0:T(8,128)(2,1)}) %reduce-scatter.55.cloned.1.call-update) | async-done | bytes 1048592 | tf_op jit(solution)/shard_map/reduce_scatter | solution.py:410
  1264.2 74.8 %reduce-scatter.81.cloned.1.call-done = bf16[128,4096]{1,0:T(8,128)(2,1)} async-done(((bf16[1024,4096]{1,0:T(8,128)(2,1)}), bf16[128,4096]{1,0:T(8,128)(2,1)}) %reduce-scatter.81.cloned.1.call-update) | async-done | bytes 1048592
  1352.8 12.3 all-reduce
  1365.2 11.7 all-reduce.1
  1377.4 26.6 %reduce-scatter.73.cloned.1.call-done = bf16[384,1024]{1,0:T(8,128)(2,1)} async-done(((bf16[3072,1024]{1,0:T(8,128)(2,1)}), bf16[384,1024]{1,0:T(8,128)(2,1)}) %reduce-scatter.73.cloned.1.call-update) | async-done | bytes 786448
  1406.3 18.3 %fusion.155 = bf16[1,4,256,1024]{3,2,1,0:T(8,128)(2,1)} fusion(f32[4,256,1024]{2,1,0:T(8,128)} %bitcast.700, f32[1024]{0:T(1024)S(1)} %bitcast.838, bf16[4096,1024]{1,0:T(8,128)(2,1)} %all-gather.29.cloned.1.call-done, f32[4,256,4096]{2,1,0:T(8,128)} %fusion.32, f32[4096]{0:T(1024)S(1)} %bitcast.827), kind=kOutput, calls=%fused_computation.206 | convolution fusion | flops 8635023360 | bytes 31477760 | tf_op jit(solution)/shard_map/dot_general | solution.py:24
  1426.9 18.1 %reduce-scatter.71.cloned.1.call-done = bf16[32,3]{1,0:T(8,128)(2,1)} async-done(((bf16[128,3]{1,0:T(8,128)(2,1)}), bf16[32,3]{1,0:T(8,128)(2,1)}) %reduce-scatter.71.cloned.1.call-update) | async-done | bytes 208
  1446.4 18.3 %reduce-scatter.67.cloned.1.call-done = bf16[32,3]{1,0:T(8,128)(2,1)} async-done(((bf16[128,3]{1,0:T(8,128)(2,1)}), bf16[32,3]{1,0:T(8,128)(2,1)}) %reduce-scatter.67.cloned.1.call-update) | async-done | bytes 208
  1466.0 18.3 %reduce-scatter.63.cloned.1.call-done = bf16[32,8]{1,0:T(8,128)(2,1)} async-done(((bf16[128,8]{1,0:T(8,128)(2,1)}), bf16[32,8]{1,0:T(8,128)(2,1)}) %reduce-scatter.63.cloned.1.call-update) | async-done | bytes 528
  1485.7 19.6 %reduce-scatter.53.cloned.1.call-done = bf16[256,128]{1,0:T(8,128)(2,1)} async-done(((bf16[1024,128]{1,0:T(8,128)(2,1)}), bf16[256,128]{1,0:T(8,128)(2,1)}) %reduce-scatter.53.cloned.1.call-update) | async-done | bytes 65552 | tf_op jit(solution)/shard_map/reduce_scatter | solution.py:454
  1506.8 19.5 %reduce-scatter.49.cloned.1.call-done = bf16[256,128]{1,0:T(8,128)(2,1)} async-done(((bf16[1024,128]{1,0:T(8,128)(2,1)}), bf16[256,128]{1,0:T(8,128)(2,1)}) %reduce-scatter.49.cloned.1.call-update) | async-done | bytes 65552 | tf_op jit(solution)/shard_map/reduce_scatter | solution.py:448
  1527.8 22.2 %reduce-scatter.51.cloned.1.call-done = bf16[256,384]{1,0:T(8,128)(2,1)} async-done(((bf16[1024,384]{1,0:T(8,128)(2,1)}), bf16[256,384]{1,0:T(8,128)(2,1)}) %reduce-scatter.51.cloned.1.call-update) | async-done | bytes 196624 | tf_op jit(solution)/shard_map/reduce_scatter | solution.py:451
  1551.7 27.3 %reduce-scatter.57.cloned.1.call-done = bf16[256,512]{1,0:T(8,128)(2,1)} async-done(((bf16[1024,512]{1,0:T(8,128)(2,1)}), bf16[256,512]{1,0:T(8,128)(2,1)}) %reduce-scatter.57.cloned.1.call-update) | async-done | bytes 262160 | tf_op jit(solution)/shard_map/reduce_scatter | solution.py:457
  1580.8 26.2 %reduce-scatter.59.cloned.1.call-done = bf16[1024,128]{1,0:T(8,128)(2,1)} async-done(((bf16[4096,128]{1,0:T(8,128)(2,1)}), bf16[1024,128]{1,0:T(8,128)(2,1)}) %reduce-scatter.59.cloned.1.call-update) | async-done | bytes 262160 | tf_op jit(solution)/shard_map/reduce_scatter | solution.py:460
  1608.7 22.2 %reduce-scatter.47.cloned.1.call-done = bf16[256,384]{1,0:T(8,128)(2,1)} async-done(((bf16[1024,384]{1,0:T(8,128)(2,1)}), bf16[256,384]{1,0:T(8,128)(2,1)}) %reduce-scatter.47.cloned.1.call-update) | async-done | bytes 196624 | tf_op jit(solution)/shard_map/reduce_scatter | solution.py:445
  (636 shorter events, 595.9 us)
Async XLA Ops:
  7.3 163.6 %copy-start.139 = (s32[1,4]{1,0:T(1,128)S(1)}, s32[1,4]{1,0:T(1,128)}, u32[]{:S(2)}) copy-start(s32[1,4]{1,0:T(1,128)} %param.19) | copy-start | bytes 52
  7.3 163.8 %copy-start.11 = (bf16[1,4,256,1024]{3,2,1,0:T(8,128)(2,1)S(1)}, bf16[1,4,256,1024]{3,2,1,0:T(8,128)(2,1)}, u32[]{:S(2)}) copy-start(bf16[1,4,256,1024]{3,2,1,0:T(8,128)(2,1)} %param.17) | copy-start | bytes 6291460
  7.3 89.6 %all-gather.23.cloned.1.call-start = ((), (), s32[]{:S(2)}) async-start(), calls=%async_computation.32 | async-start | bytes 1310720 | tf_op jit(solution)/shard_map/all_gather | solution.py:213
  8.0 165.6 %all-gather.27.cloned.1.call-start = ((), (), s32[]{:S(2)}) async-start(), calls=%async_computation.34 | async-start | bytes 1310720 | tf_op jit(solution)/shard_map/all_gather | solution.py:214
  8.8 164.9 %all-gather.15.cloned.1.call-start = ((), (), s32[]{:S(2)}) async-start(), calls=%async_computation.28 | async-start | bytes 7077888 | tf_op jit(solution)/shard_map/all_gather | solution.py:234
  35.9 163.2 %all-gather.17.cloned.1.call-start = ((), (), s32[]{:S(2)}) async-start(), calls=%async_computation.29 | async-start | bytes 2359296 | tf_op jit(solution)/shard_map/all_gather | solution.py:235
  54.1 207.5 %all-gather.19.cloned.1.call-start = ((), (), s32[]{:S(2)}) async-start(), calls=%async_computation.30 | async-start | bytes 7077888 | tf_op jit(solution)/shard_map/all_gather | solution.py:236
  80.7 208.7 %all-gather.21.cloned.1.call-start = ((), (), s32[]{:S(2)}) async-start(), calls=%async_computation.31 | async-start | bytes 2359296 | tf_op jit(solution)/shard_map/all_gather | solution.py:237
  96.8 336.6 %all-gather.25.cloned.1.call-start = ((), (), s32[]{:S(2)}) async-start(), calls=%async_computation.33 | async-start | bytes 9437184 | tf_op jit(solution)/shard_map/all_gather | solution.py:238
  97.5 343.9 %all-gather.29.cloned.1.call-start = ((), (), s32[]{:S(2)}) async-start(), calls=%async_computation.35 | async-start | bytes 9437184 | tf_op jit(solution)/shard_map/all_gather | solution.py:239
  173.0 361.5 %copy-start.79 = (f32[1,1024]{1,0:T(1,128)}, f32[1,1024]{1,0:T(1,128)S(1)}, u32[]{:S(2)}) copy-start(f32[1,1024]{1,0:T(1,128)S(1)} %get-tuple-element.61) | copy-start | bytes 12292
  173.0 446.3 %copy-start.73 = (f32[1,1024]{1,0:T(1,128)}, f32[1,1024]{1,0:T(1,128)S(1)}, u32[]{:S(2)}) copy-start(f32[1,1024]{1,0:T(1,128)S(1)} %get-tuple-element.60) | copy-start | bytes 12292
  173.0 202.9 %copy-start.128 = (f32[1,1024]{1,0:T(1,128)}, f32[1,1024]{1,0:T(1,128)S(1)}, u32[]{:S(2)}) copy-start(f32[1,1024]{1,0:T(1,128)S(1)} %get-tuple-element.64) | copy-start | bytes 12292
  173.0 388.4 %copy-start.101 = (f32[1,1024]{1,0:T(1,128)}, f32[1,1024]{1,0:T(1,128)S(1)}, u32[]{:S(2)}) copy-start(f32[1,1024]{1,0:T(1,128)S(1)} %get-tuple-element.63) | copy-start | bytes 12292
  203.0 53.9 %all-to-all-start.2 = ((bf16[1,4,64,1024]{3,1,0,2:T(4,128)(2,1)}), bf16[1,4,64,1024]{3,1,0,2:T(4,128)(2,1)S(1)}, u32[]{:S(2)}, u32[]{:S(2)}) async-start(bf16[1,4,64,1024]{3,1,0,2:T(4,128)(2,1)} %copy.378), calls=%async_computation.2 | async-start | bytes 1048576 | tf_op jit(solution)/shard_map/all_to_all | solution.py:276
  260.4 274.1 %copy-start.84 = (f32[16,16]{1,0:T(8,128)}, f32[16,16]{1,0:T(8,128)S(1)}, u32[]{:S(2)}) copy-start(f32[16,16]{1,0:T(8,128)S(1)} %rsqrt.82) | copy-start | bytes 3076
  292.8 19.9 %all-to-all-start.3 = ((bf16[1,16,16,1024]{3,2,0,1:T(8,128)(2,1)}), bf16[1,16,16,1024]{3,2,0,1:T(8,128)(2,1)S(1)}, u32[]{:S(2)}, u32[]{:S(2)}) async-start(bf16[1,16,16,1024]{3,2,0,1:T(8,128)(2,1)} %fusion.212), calls=%async_computation.3 | async-start | bytes 1048576 | tf_op jit(solution)/shard_map/all_to_all | solution.py:297
  312.7 55.3 %all-to-all-start = ((bf16[1,4,256,1024]{3,1,0,2:T(4,128)(2,1)}), bf16[1,4,256,1024]{3,1,0,2:T(4,128)(2,1)S(1)}, u32[]{:S(2)}, u32[]{:S(2)}) async-start(bf16[1,4,256,1024]{3,1,0,2:T(4,128)(2,1)} %copy.357), calls=%async_computation | async-start | bytes 4194304 | tf_op jit(solution)/shard_map/all_to_all | solution.py:275
  364.5 213.3 %copy-start.120 = (f32[8,1,512]{2,1,0:T(1,128)}, f32[8,1,512]{2,1,0:T(1,128)S(1)}, u32[]{:S(2)}) copy-start(f32[8,1,512]{2,1,0:T(1,128)S(1)} %convert_element_type.666) | copy-start | bytes 49156
  458.7 36.7 %all-to-all-start.6 = ((bf16[1,4,64,1024]{3,1,0,2:T(4,128)(2,1)}), bf16[1,4,64,1024]{3,1,0,2:T(4,128)(2,1)S(1)}, u32[]{:S(2)}, u32[]{:S(2)}) async-start(bf16[1,4,64,1024]{3,1,0,2:T(4,128)(2,1)} %copy.407), calls=%async_computation.6 | async-start | bytes 1048576 | tf_op jit(solution)/shard_map/all_to_all | solution.py:323
  495.4 53.4 %all-to-all-start.1 = ((bf16[1,16,64,1024]{3,2,0,1:T(8,128)(2,1)}), bf16[1,16,64,1024]{3,2,0,1:T(8,128)(2,1)S(1)}, u32[]{:S(2)}, u32[]{:S(2)}) async-start(bf16[1,16,64,1024]{3,2,0,1:T(8,128)(2,1)} %fusion.162), calls=%async_computation.1 | async-start | bytes 4194304 | tf_op jit(solution)/shard_map/all_to_all | solution.py:296
  548.9 75.3 %all-to-all-start.7 = ((bf16[1,16,16,1024]{3,2,0,1:T(8,128)(2,1)}), bf16[1,16,16,1024]{3,2,0,1:T(8,128)(2,1)S(1)}, u32[]{:S(2)}, u32[]{:S(2)}) async-start(bf16[1,16,16,1024]{3,2,0,1:T(8,128)(2,1)} %fusion.248), calls=%async_computation.7 | async-start | bytes 1048576 | tf_op jit(solution)/shard_map/all_to_all | solution.py:344
  624.2 52.4 %all-to-all-start.4 = ((bf16[1,4,256,1024]{3,1,0,2:T(4,128)(2,1)}), bf16[1,4,256,1024]{3,1,0,2:T(4,128)(2,1)S(1)}, u32[]{:S(2)}, u32[]{:S(2)}) async-start(bf16[1,4,256,1024]{3,1,0,2:T(4,128)(2,1)} %copy.388), calls=%async_computation.4 | async-start | bytes 4194304 | tf_op jit(solution)/shard_map/all_to_all | solution.py:322
  780.7 52.5 %all-to-all-start.5 = ((bf16[1,16,64,1024]{3,2,0,1:T(8,128)(2,1)}), bf16[1,16,64,1024]{3,2,0,1:T(8,128)(2,1)}, u32[]{:S(2)}, u32[]{:S(2)}) async-start(bf16[1,16,64,1024]{3,2,0,1:T(8,128)(2,1)} %fusion.112), calls=%async_computation.5 | async-start | bytes 4194304 | tf_op jit(solution)/shard_map/all_to_all | solution.py:343
  785.4 296.3 %reduce-scatter.83.cloned.1.call-start = ((), (), s32[]{:S(2)}) async-start(), calls=%async_computation.54 | async-start | bytes 294912
  891.6 190.8 %reduce-scatter.69.cloned.1.call-start = ((), (), s32[]{:S(2)}) async-start(), calls=%async_computation.47 | async-start | bytes 294912
  927.4 155.6 %reduce-scatter.65.cloned.1.call-start = ((), (), s32[]{:S(2)}) async-start(), calls=%async_computation.45 | async-start | bytes 294912
  928.4 155.4 %reduce-scatter.61.cloned.1.call-start = ((), (), s32[]{:S(2)}) async-start(), calls=%async_computation.43 | async-start | bytes 294912
  929.6 154.9 %reduce-scatter.79.cloned.1.call-start = ((), (), s32[]{:S(2)}) async-start(), calls=%async_computation.52 | async-start | bytes 2359296
  935.2 189.3 %reduce-scatter.75.cloned.1.call-start = ((), (), s32[]{:S(2)}) async-start(), calls=%async_computation.50 | async-start | bytes 2359296
  950.8 238.7 %reduce-scatter.77.cloned.1.call-start = ((), (), s32[]{:S(2)}) async-start(), calls=%async_computation.51 | async-start | bytes 7077888
  975.1 289.0 %reduce-scatter.55.cloned.1.call-start = ((), (), s32[]{:S(2)}) async-start(), calls=%async_computation.40 | async-start | bytes 9437184 | tf_op jit(solution)/shard_map/reduce_scatter | solution.py:410
  1004.5 334.5 %reduce-scatter.81.cloned.1.call-start = ((), (), s32[]{:S(2)}) async-start(), calls=%async_computation.53 | async-start | bytes 9437184
  1047.3 356.7 %reduce-scatter.73.cloned.1.call-start = ((), (), s32[]{:S(2)}) async-start(), calls=%async_computation.49 | async-start | bytes 7077888
  1081.6 260.0 %copy-start.142 = (u32[32]{0:T(128)S(1)}, u32[32]{0:T(128)}, u32[]{:S(2)}) copy-start(u32[32]{0:T(128)} %constant.80) | copy-start | bytes 388
  1081.6 260.6 %copy-start.141 = (u32[32]{0:T(128)S(1)}, u32[32]{0:T(128)}, u32[]{:S(2)}) copy-start(u32[32]{0:T(128)} %constant.84) | copy-start | bytes 388
  1081.6 262.4 %copy-start.22 = (f32[1,4,4,16,1024]{4,3,1,2,0:T(8,128)S(1)}, f32[1,4,4,16,1024]{4,3,1,2,0:T(8,128)}, u32[]{:S(2)}) copy-start(f32[1,4,4,16,1024]{4,3,1,2,0:T(8,128)} %copy.387) | copy-start | bytes 3145732
  1081.6 262.4 %copy-start.125 = (f32[1,1024]{1,0:T(1,128)S(1)}, f32[1,1024]{1,0:T(1,128)}, u32[]{:S(2)}) copy-start(f32[1,1024]{1,0:T(1,128)} %get-tuple-element.66) | copy-start | bytes 12292
  1081.6 343.9 %reduce-scatter.85.cloned.1.call-start = ((), (), s32[]{:S(2)}) async-start(), calls=%async_computation.55 | async-start | bytes 40960
  1082.4 362.6 %reduce-scatter.71.cloned.1.call-start = ((), (), s32[]{:S(2)}) async-start(), calls=%async_computation.48 | async-start | bytes 40960
  1083.0 381.7 %reduce-scatter.67.cloned.1.call-start = ((), (), s32[]{:S(2)}) async-start(), calls=%async_computation.46 | async-start | bytes 40960
  1083.7 400.6 %reduce-scatter.63.cloned.1.call-start = ((), (), s32[]{:S(2)}) async-start(), calls=%async_computation.44 | async-start | bytes 40960
  1084.5 420.8 %reduce-scatter.53.cloned.1.call-start = ((), (), s32[]{:S(2)}) async-start(), calls=%async_computation.39 | async-start | bytes 327680 | tf_op jit(solution)/shard_map/reduce_scatter | solution.py:454
  1086.3 439.9 %reduce-scatter.49.cloned.1.call-start = ((), (), s32[]{:S(2)}) async-start(), calls=%async_computation.37 | async-start | bytes 327680 | tf_op jit(solution)/shard_map/reduce_scatter | solution.py:448
  1126.3 423.7 %reduce-scatter.51.cloned.1.call-start = ((), (), s32[]{:S(2)}) async-start(), calls=%async_computation.38 | async-start | bytes 983040 | tf_op jit(solution)/shard_map/reduce_scatter | solution.py:451
  1191.8 387.2 %reduce-scatter.57.cloned.1.call-start = ((), (), s32[]{:S(2)}) async-start(), calls=%async_computation.41 | async-start | bytes 1310720 | tf_op jit(solution)/shard_map/reduce_scatter | solution.py:457
  1264.2 342.8 %reduce-scatter.59.cloned.1.call-start = ((), (), s32[]{:S(2)}) async-start(), calls=%async_computation.42 | async-start | bytes 1310720 | tf_op jit(solution)/shard_map/reduce_scatter | solution.py:460
  1341.3 289.7 %reduce-scatter.47.cloned.1.call-start = ((), (), s32[]{:S(2)}) async-start(), calls=%async_computation.36 | async-start | bytes 983040 | tf_op jit(solution)/shard_map/reduce_scatter | solution.py:445
  (138 other events, 2094.9 us)
Sparse Core Ops, SparseCore 0:
  9.7 39.3 all-gather.22
  50.6 37.1 all-gather.26
  89.7 46.4 all-gather.14
  137.9 28.0 all-gather.16
  167.8 46.5 all-gather.18
  216.1 28.0 all-gather.20
  246.1 55.8 all-gather.24
  303.9 55.8 all-gather.28
  891.7 32.3 reduce-scatter.82
  927.6 33.6 reduce-scatter.68
  964.9 33.6 reduce-scatter.64
  1002.1 33.6 reduce-scatter.60
  1039.1 41.0 reduce-scatter.78
  1083.3 41.1 reduce-scatter.74
  1127.7 61.7 reduce-scatter.76
  1192.8 71.2 reduce-scatter.54
  1267.4 71.4 reduce-scatter.80
  1342.2 61.7 reduce-scatter.72
  1406.2 19.2 reduce-scatter.84
  1427.6 17.3 reduce-scatter.70
  1447.2 17.3 reduce-scatter.66
  1466.9 17.3 reduce-scatter.62
  1487.1 18.1 reduce-scatter.52
  1508.0 18.2 reduce-scatter.48
  1528.6 21.3 reduce-scatter.50
  1552.1 26.7 reduce-scatter.56
  1581.1 25.7 reduce-scatter.58
  1609.2 21.6 reduce-scatter.46
where the time goes:
time: 1650 us; the launch traced here: 1640 us
  waiting for transfers between devices  539 us (33%)
  matrix products  441 us (27%)
  local copies, waits for them, and re-layouts  243 us (15%)
  blocking collectives  231 us (14%)
  other arithmetic  120 us (7%)
  starting transfers between devices  47.2 us (3%)
  between operations  18.3 us (1%)
    unnamed x41, waiting for transfers between devices  263 us
    dot_general x12, matrix products, outer_sum(): lax.dot_general(flat_left, flat_right, (((0,), (0,)), ((), ())), preferre...  108 us
    dot_general x12, matrix products, through(): lax.dot_general(gradient, weight, (((gradient.ndim - 1,), (1,)), ((), ())...  103 us
    dot_general x12, matrix products, project(): return jnp.dot(activation, weight, preferred_element_type=jnp.float32)  98.7 us
    unnamed x327, local copies, waits for them, and re-layouts  74.9 us
    reduce_scatter x1, waiting for transfers between devices, body(): lax.psum_scatter(grad_up.astype(jnp.bfloat16), 'clip', scatter_dimension=...  72.3 us
    reshape x12, local copies, waits for them, and re-layouts, from_sequences(): tensor.reshape((leading[0], leading[2], leading[1], -1))  43.2 us
    all_gather x1, blocking collectives, body(): lax.all_gather(hidden_bias, 'frame', axis=0, tiled=True)  39.5 us
  transfers between devices with their start and end apart: 36, of which 19 were waited for; matrix products, arithmetic and copies ran while one was open for 37% of the time, Pallas kernels for 0%

commit v1 on v0

--- a/solution.py
+++ b/solution.py
@@ -3,7 +3,509 @@
 import jax
 import jax.numpy as jnp
 from jax import lax
+from jax.experimental import pallas as pl
+from jax.experimental.pallas import tpu as pltpu
 from jax.sharding import PartitionSpec as P
+
+F32 = jnp.float32
+BF16 = jnp.bfloat16
+D = 1024
+ROWS = 256
+NEG = -1e30
+EPS = 1e-05
+VMEM_BYTES = 60 * 1024 * 1024
+
+
+def nn(left, right):
+    return lax.dot_general(left, right, (((1,), (0,)), ((), ())), preferred_element_type=F32)
+
+
+def nt(left, right):
+    return lax.dot_general(left, right, (((1,), (1,)), ((), ())), preferred_element_type=F32)
+
+
+def tn(left, right):
+    return lax.dot_general(left, right, (((0,), (0,)), ((), ())), preferred_element_type=F32)
+
+
+def normal_parts(values):
+    center = values - jnp.mean(values, axis=-1, keepdims=True)
+    scale = lax.rsqrt(jnp.mean(center * center, axis=-1, keepdims=True) + EPS)
+    return center * scale, scale
+
+
+def normal_back(grad, normed, scale, gain):
+    scaled = grad * gain
+    first = jnp.mean(scaled, axis=-1, keepdims=True)
+    second = jnp.mean(scaled * normed, axis=-1, keepdims=True)
+    return scale * (scaled - first - normed * second)
+
+
+def weight_copies(source, target, sems, width, base=0):
+    blocks = source.shape[0]
+    return [
+        pltpu.make_async_copy(
+            source.at[c], target.at[:, c * width : (c + 1) * width], sems.at[base + c]
+        )
+        for c in range(blocks)
+    ]
+
+
+def score_bias(spatial, step):
+    rows = lax.broadcasted_iota(jnp.int32, (ROWS, ROWS), 0)
+    cols = lax.broadcasted_iota(jnp.int32, (ROWS, ROWS), 1)
+    if spatial:
+        apart = jnp.logical_and((rows // 64) != (cols // 64), step == 4)
+        return jnp.where(apart, NEG, 0.0)
+    seen = jnp.logical_and(rows % 16 == cols % 16, rows // 16 >= cols // 16)
+    return jnp.where(seen, 0.0, NEG)
+
+
+def fwd_kernel(spatial, *refs):
+    if spatial:
+        x_ref, e_ref, small_ref, win_hbm, wo_hbm = refs[:5]
+        refs = refs[5:]
+    else:
+        x_ref, small_ref, win_hbm, wo_hbm = refs[:4]
+        refs = refs[4:]
+    y_ref, qkv_ref, o_ref, lse_ref, win, wo, bias_s, sems = refs
+    step = pl.program_id(0)
+    copies_in = weight_copies(win_hbm, win, sems, 384)
+    copies_out = weight_copies(wo_hbm, wo, sems, 128, 8)
+
+    @pl.when(step == 0)
+    def _():
+        for copy in copies_in + copies_out:
+            copy.start()
+
+    if spatial:
+        tokens = x_ref[0].astype(F32).reshape(4, 64, D)
+        start = (tokens + e_ref[0][:, None, :]).reshape(ROWS, D)
+        bias_s[...] = score_bias(True, step)
+    else:
+        start = x_ref[...].reshape(ROWS, D).astype(F32)
+
+        @pl.when(step == 0)
+        def _():
+            bias_s[...] = score_bias(False, step)
+
+    normed, _ = normal_parts(start)
+    hidden = (normed * small_ref[0:1, :] + small_ref[1:2, :]).astype(BF16)
+
+    @pl.when(step == 0)
+    def _():
+        for copy in copies_in + copies_out:
+            copy.wait()
+
+    for part in range(3):
+        qkv_ref[0, :, part * D : (part + 1) * D] = nn(
+            hidden, win[:, part * D : (part + 1) * D]
+        ).astype(BF16)
+    low = lax.broadcasted_iota(jnp.int32, (ROWS, 128), 1) < 64
+    lane = lax.broadcasted_iota(jnp.int32, (ROWS, 128), 1)
+    lse_all = jnp.zeros((ROWS, 128), F32)
+    zero = jnp.zeros((ROWS, 128), BF16)
+    for pair in range(8):
+        at = pair * 128
+        q2 = qkv_ref[0, :, at : at + 128] * jnp.asarray(0.125, BF16)
+        k2 = qkv_ref[0, :, D + at : D + at + 128]
+        v2 = qkv_ref[0, :, 2 * D + at : 2 * D + at + 128]
+        mixed = []
+        for half in range(2):
+            qh = jnp.where(low, q2, zero) if half == 0 else jnp.where(low, zero, q2)
+            scores = nt(qh, k2) + bias_s[...]
+            top = jnp.max(scores, axis=-1, keepdims=True)
+            expo = jnp.exp(scores - top)
+            total = jnp.sum(expo, axis=-1, keepdims=True)
+            mixed.append(nn(expo.astype(BF16), v2) * (1.0 / total))
+            lse_all = jnp.where(lane == 2 * pair + half, top + jnp.log(total), lse_all)
+        o_ref[0, :, at : at + 128] = jnp.where(low, mixed[0], mixed[1]).astype(BF16)
+    lse_ref[0] = lse_all
+    result = (start + (nn(o_ref[0], wo[...]) + small_ref[2:3, :])).astype(BF16)
+    if spatial:
+
+        @pl.when(step < 4)
+        def _():
+            y_ref[:, 0:4, step, :, :] = result.reshape(4, 4, 16, D)
+
+        @pl.when(step == 4)
+        def _():
+            parts = result.reshape(4, 4, 16, D)
+            for j in range(4):
+                y_ref[j, 4, :, :, :] = parts[:, j]
+    else:
+        y_ref[...] = result.reshape(4, 1, 64, D)
+
+
+def attention_forward(spatial, x, embed, small, win, wo):
+    whole = pl.BlockSpec(memory_space=pl.ANY)
+    small_spec = pl.BlockSpec((8, D), lambda s: (0, 0))
+    if spatial:
+        in_specs = [
+            pl.BlockSpec((1, ROWS, D), lambda s: (s, 0, 0)),
+            pl.BlockSpec((1, 4, D), lambda s: (s, 0, 0)),
+            small_spec,
+            whole,
+            whole,
+        ]
+        operands = (x, embed, small, win, wo)
+        y_spec = pl.BlockSpec((4, 5, 4, 16, D), lambda s: (0, 0, 0, 0, 0))
+        y_shape = (4, 5, 4, 16, D)
+    else:
+        in_specs = [
+            pl.BlockSpec((4, 1, 64, D), lambda s: (0, s, 0, 0)),
+            small_spec,
+            whole,
+            whole,
+        ]
+        operands = (x, small, win, wo)
+        y_spec = pl.BlockSpec((4, 1, 64, D), lambda s: (0, s, 0, 0))
+        y_shape = (4, 5, 64, D)
+    return pl.pallas_call(
+        partial(fwd_kernel, spatial),
+        grid=(5,),
+        in_specs=in_specs,
+        out_specs=[
+            y_spec,
+            pl.BlockSpec((1, ROWS, 3 * D), lambda s: (s, 0, 0)),
+            pl.BlockSpec((1, ROWS, D), lambda s: (s, 0, 0)),
+            pl.BlockSpec((1, ROWS, 128), lambda s: (s, 0, 0)),
+        ],
+        out_shape=[
+            jax.ShapeDtypeStruct(y_shape, BF16),
+            jax.ShapeDtypeStruct((5, ROWS, 3 * D), BF16),
+            jax.ShapeDtypeStruct((5, ROWS, D), BF16),
+            jax.ShapeDtypeStruct((5, ROWS, 128), F32),
+        ],
+        scratch_shapes=[
+            pltpu.VMEM((D, 3 * D), BF16),
+            pltpu.VMEM((D, D), BF16),
+            pltpu.VMEM((ROWS, ROWS), F32),
+            pltpu.SemaphoreType.DMA((16,)),
+        ],
+        compiler_params=pltpu.CompilerParams(
+            dimension_semantics=("arbitrary",), vmem_limit_bytes=VMEM_BYTES
+        ),
+        cost_estimate=pl.CostEstimate(
+            flops=2 * 1280 * D * 4 * D, bytes_accessed=30 * 1024 * 1024, transcendentals=5242880
+        ),
+        name="spatial_fwd" if spatial else "temporal_fwd",
+    )(*operands)
+
+
+def bwd_kernel(spatial, *refs):
+    if spatial:
+        g_ref, x_ref, e_ref, small_ref, qkv_ref, lse_ref, win_hbm, wo_hbm = refs[:8]
+        big_ref, small_out_ref, frame_ref, h_ref, dqkv_ref, dy_ref, sums_ref = refs[8:15]
+        win, wo, bias_s, do_s, sems = refs[15:]
+    else:
+        g_ref, x_ref, small_ref, qkv_ref, lse_ref, win_hbm, wo_hbm = refs[:7]
+        dx_ref, h_ref, dqkv_ref, sums_ref = refs[7:11]
+        win, wo, bias_s, do_s, sems = refs[11:]
+    step = pl.program_id(0)
+    copies_in = weight_copies(win_hbm, win, sems, 384)
+    copies_out = weight_copies(wo_hbm, wo, sems, 128, 8)
+
+    @pl.when(step == 0)
+    def _():
+        for copy in copies_in + copies_out:
+            copy.start()
+        sums_ref[...] = jnp.zeros((8, D), F32)
+
+    if spatial:
+        bias_s[...] = score_bias(True, step)
+
+        @pl.when(step < 4)
+        def _():
+            dy_ref[0] = g_ref[:, 0:4, step, :, :].reshape(ROWS, D)
+
+        @pl.when(step == 4)
+        def _():
+            for j in range(4):
+                for f in range(4):
+                    dy_ref[0, f * 64 + j * 16 : f * 64 + (j + 1) * 16, :] = g_ref[j, 4, f, :, :]
+
+        grad = dy_ref[0]
+    else:
+        grad = g_ref[...].reshape(ROWS, D)
+
+        @pl.when(step == 0)
+        def _():
+            bias_s[...] = score_bias(False, step)
+
+    @pl.when(step == 0)
+    def _():
+        for copy in copies_in + copies_out:
+            copy.wait()
+
+    do_s[...] = nt(grad, wo[...]).astype(BF16)
+    low = lax.broadcasted_iota(jnp.int32, (ROWS, 128), 1) < 64
+    zero = jnp.zeros((ROWS, 128), BF16)
+    eighth = jnp.asarray(0.125, BF16)
+
+    def halves(value):
+        return jnp.where(low, value, zero), jnp.where(low, zero, value)
+
+    for pair in range(8):
+        at = pair * 128
+        q2 = halves(qkv_ref[0, :, at : at + 128] * eighth)
+        k2 = qkv_ref[0, :, D + at : D + at + 128]
+        kh = halves(k2 * eighth)
+        v2 = qkv_ref[0, :, 2 * D + at : 2 * D + at + 128]
+        do2 = halves(do_s[:, at : at + 128])
+        dq = dk = dv = None
+        for half in range(2):
+            index = 2 * pair + half
+            probs = jnp.exp(nt(q2[half], k2) + bias_s[...] - lse_ref[0, :, index : index + 1])
+            dprobs = nt(do2[half], v2)
+            inner = jnp.sum(probs * dprobs, axis=-1, keepdims=True)
+            dscores = (probs * (dprobs - inner)).astype(BF16)
+            dv_h = tn(probs.astype(BF16), do2[half])
+            dk_h = tn(dscores, q2[half])
+            dq_h = nn(dscores, kh[half])
+            dq = dq_h if dq is None else dq + dq_h
+            dk = dk_h if dk is None else dk + dk_h
+            dv = dv_h if dv is None else dv + dv_h
+        dqkv_ref[0, :, at : at + 128] = dq.astype(BF16)
+        dqkv_ref[0, :, D + at : D + at + 128] = dk.astype(BF16)
+        dqkv_ref[0, :, 2 * D + at : 2 * D + at + 128] = dv.astype(BF16)
+    dh = nt(dqkv_ref[0], win[...])
+    if spatial:
+        tokens = x_ref[0].astype(F32).reshape(4, 64, D)
+        start = (tokens + e_ref[0][:, None, :]).reshape(ROWS, D)
+    else:
+        start = x_ref[...].reshape(ROWS, D).astype(F32)
+    normed, scale = normal_parts(start)
+    gain = small_ref[0:1, :]
+    h_ref[0] = (normed * gain + small_ref[1:2, :]).astype(BF16)
+    grad32 = grad.astype(F32)
+    total = grad32 + normal_back(dh, normed, scale, gain)
+    sums_ref[0:1, :] += jnp.sum(dh * normed, axis=0, keepdims=True)
+    sums_ref[1:2, :] += jnp.sum(dh, axis=0, keepdims=True)
+    sums_ref[2:3, :] += jnp.sum(grad32, axis=0, keepdims=True)
+    if spatial:
+        frame_ref[0] = jnp.sum(total.reshape(4, 64, D), axis=1)
+
+        @pl.when(step < 4)
+        def _():
+            big_ref[0] = total
+
+        @pl.when(step == 4)
+        def _():
+            small_out_ref[...] = total
+    else:
+        dx_ref[...] = total.astype(BF16).reshape(4, 1, 64, D)
+
+
+def attention_backward(spatial, grad, x, embed, small, qkv, lse, win, wo):
+    whole = pl.BlockSpec(memory_space=pl.ANY)
+    small_spec = pl.BlockSpec((8, D), lambda s: (0, 0))
+    row_spec = pl.BlockSpec((1, ROWS, D), lambda s: (s, 0, 0))
+    wide_spec = pl.BlockSpec((1, ROWS, 3 * D), lambda s: (s, 0, 0))
+    lse_spec = pl.BlockSpec((1, ROWS, 128), lambda s: (s, 0, 0))
+    group_spec = pl.BlockSpec((4, 1, 64, D), lambda s: (0, s, 0, 0))
+    sums_spec = pl.BlockSpec((8, D), lambda s: (0, 0))
+    rows_shape = jax.ShapeDtypeStruct((5, ROWS, D), BF16)
+    wide_shape = jax.ShapeDtypeStruct((5, ROWS, 3 * D), BF16)
+    sums_shape = jax.ShapeDtypeStruct((8, D), F32)
+    if spatial:
+        in_specs = [
+            pl.BlockSpec((4, 5, 4, 16, D), lambda s: (0, 0, 0, 0, 0)),
+            row_spec,
+            pl.BlockSpec((1, 4, D), lambda s: (s, 0, 0)),
+            small_spec,
+            wide_spec,
+            lse_spec,
+            whole,
+            whole,
+        ]
+        operands = (grad, x, embed, small, qkv, lse, win, wo)
+        out_specs = [
+            pl.BlockSpec((1, ROWS, D), lambda s: (jnp.minimum(s, 3), 0, 0)),
+            pl.BlockSpec((ROWS, D), lambda s: (0, 0)),
+            pl.BlockSpec((1, 4, D), lambda s: (s, 0, 0)),
+            row_spec,
+            wide_spec,
+            row_spec,
+            sums_spec,
+        ]
+        out_shape = [
+            jax.ShapeDtypeStruct((4, ROWS, D), F32),
+            jax.ShapeDtypeStruct((ROWS, D), F32),
+            jax.ShapeDtypeStruct((5, 4, D), F32),
+            rows_shape,
+            wide_shape,
+            rows_shape,
+            sums_shape,
+        ]
+    else:
+        in_specs = [group_spec, group_spec, small_spec, wide_spec, lse_spec, whole, whole]
+        operands = (grad, x, small, qkv, lse, win, wo)
+        out_specs = [group_spec, row_spec, wide_spec, sums_spec]
+        out_shape = [
+            jax.ShapeDtypeStruct((4, 5, 64, D), BF16),
+            rows_shape,
+            wide_shape,
+            sums_shape,
+        ]
+    return pl.pallas_call(
+        partial(bwd_kernel, spatial),
+        grid=(5,),
+        in_specs=in_specs,
+        out_specs=out_specs,
+        out_shape=out_shape,
+        scratch_shapes=[
+            pltpu.VMEM((D, 3 * D), BF16),
+            pltpu.VMEM((D, D), BF16),
+            pltpu.VMEM((ROWS, ROWS), F32),
+            pltpu.VMEM((ROWS, D), BF16),
+            pltpu.SemaphoreType.DMA((16,)),
+        ],
+        compiler_params=pltpu.CompilerParams(
+            dimension_semantics=("arbitrary",), vmem_limit_bytes=VMEM_BYTES
+        ),
+        cost_estimate=pl.CostEstimate(
+            flops=2 * 1280 * D * 4 * D, bytes_accessed=40 * 1024 * 1024, transcendentals=5242880
+        ),
+        name="spatial_bwd" if spatial else "temporal_bwd",
+    )(*operands)
+
+
+GELU_A = 0.7978845608028654
+GELU_B = 0.044715
+FF_CHUNK = 512
+
+
+def ffn_kernel(x_ref, g_ref, small_ref, hb_ref, up_hbm, down_hbm, out_ref, dx_ref, h_ref, act_ref, du_ref, sums_ref, hsum_ref, up, down, acc, dacc, sems):
+    step = pl.program_id(0)
+    copies = weight_copies(up_hbm, up, sems, 512) + weight_copies(down_hbm, down, sems, 128, 8)
+
+    @pl.when(step == 0)
+    def _():
+        for copy in copies:
+            copy.start()
+        sums_ref[...] = jnp.zeros((8, D), F32)
+        hsum_ref[...] = jnp.zeros((1, 4 * D), F32)
+
+    start = x_ref[...].astype(F32)
+    normed, scale = normal_parts(start)
+    gain = small_ref[0:1, :]
+    hidden = (normed * gain + small_ref[1:2, :]).astype(BF16)
+    h_ref[...] = hidden
+    grad = g_ref[...]
+
+    @pl.when(step == 0)
+    def _():
+        for copy in copies:
+            copy.wait()
+
+    for chunk in range(4 * D // FF_CHUNK):
+        cols = slice(chunk * FF_CHUNK, (chunk + 1) * FF_CHUNK)
+        u = nn(hidden, up[:, cols]) + hb_ref[:, cols]
+        dact = nt(grad, down[cols, :])
+        square = u * u
+        inner = GELU_A * (u + GELU_B * (square * u))
+        tanh = jnp.tanh(inner)
+        half = 0.5 * (1.0 + tanh)
+        act = (u * half).astype(BF16)
+        slope = half + (0.5 * u) * (1.0 - tanh * tanh) * (GELU_A + (3.0 * GELU_A * GELU_B) * square)
+        du = (slope * dact).astype(BF16)
+        act_ref[:, cols] = act
+        du_ref[:, cols] = du
+        hsum_ref[:, cols] += jnp.sum(du.astype(F32), axis=0, keepdims=True)
+    out_ref[...] = (start + (nn(act_ref[...], down[...]) + small_ref[2:3, :])).astype(BF16)
+    dh = nt(du_ref[...], up[...])
+    grad32 = grad.astype(F32)
+    dx_ref[...] = (grad32 + normal_back(dh, normed, scale, gain)).astype(BF16)
+    sums_ref[0:1, :] += jnp.sum(dh * normed, axis=0, keepdims=True)
+    sums_ref[1:2, :] += jnp.sum(dh, axis=0, keepdims=True)
+    sums_ref[2:3, :] += jnp.sum(grad32, axis=0, keepdims=True)
+
+
+def ffn(x, grad, small, hidden_bias, up, down):
+    rows = x.shape[0]
+    tile = pl.BlockSpec((ROWS, D), lambda s: (s, 0))
+    wide = pl.BlockSpec((ROWS, 4 * D), lambda s: (s, 0))
+    whole = pl.BlockSpec(memory_space=pl.ANY)
+    flat = jax.ShapeDtypeStruct((rows, D), BF16)
+    wide_shape = jax.ShapeDtypeStruct((rows, 4 * D), BF16)
+    return pl.pallas_call(
+        ffn_kernel,
+        grid=(rows // ROWS,),
+        in_specs=[
+            tile,
+            tile,
+            pl.BlockSpec((8, D), lambda s: (0, 0)),
+            pl.BlockSpec((1, 4 * D), lambda s: (0, 0)),
+            whole,
+            whole,
+        ],
+        out_specs=[
+            tile,
+            tile,
+            tile,
+            wide,
+            wide,
+            pl.BlockSpec((8, D), lambda s: (0, 0)),
+            pl.BlockSpec((1, 4 * D), lambda s: (0, 0)),
+        ],
+        out_shape=[
+            flat,
+            flat,
+            flat,
+            wide_shape,
+            wide_shape,
+            jax.ShapeDtypeStruct((8, D), F32),
+            jax.ShapeDtypeStruct((1, 4 * D), F32),
+        ],
+        scratch_shapes=[
+            pltpu.VMEM((D, 4 * D), BF16),
+            pltpu.VMEM((4 * D, D), BF16),
+            pltpu.VMEM((8, 128), F32),
+            pltpu.VMEM((8, 128), F32),
+            pltpu.SemaphoreType.DMA((16,)),
+        ],
+        compiler_params=pltpu.CompilerParams(
+            dimension_semantics=("arbitrary",), vmem_limit_bytes=VMEM_BYTES
+        ),
+        cost_estimate=pl.CostEstimate(
+            flops=8 * rows * D * 4 * D, bytes_accessed=50 * 1024 * 1024, transcendentals=5242880
+        ),
+        name="ffn",
+    )(x, grad, small, hidden_bias, up, down)
+
+
+def outer_kernel(left_ref, right_ref, out_ref):
+    product = tn(left_ref[...], right_ref[...])
+    blocks, _, width = out_ref.shape
+    for c in range(blocks):
+        out_ref[c] = product[:, c * width : (c + 1) * width].astype(BF16)
+
+
+def outer(left, right, blocks, tile, name):
+    rows, height = left.shape
+    width = right.shape[1]
+    each = width // blocks
+    return pl.pallas_call(
+        outer_kernel,
+        grid=(height // tile,),
+        in_specs=[
+            pl.BlockSpec((rows, tile), lambda s: (0, s)),
+            pl.BlockSpec((rows, width), lambda s: (0, 0)),
+        ],
+        out_specs=pl.BlockSpec((blocks, tile, each), lambda s: (0, s, 0)),
+        out_shape=jax.ShapeDtypeStruct((blocks, height, each), BF16),
+        compiler_params=pltpu.CompilerParams(
+            dimension_semantics=("arbitrary",), vmem_limit_bytes=VMEM_BYTES
+        ),
+        cost_estimate=pl.CostEstimate(
+            flops=2 * rows * height * width,
+            bytes_accessed=2 * (rows * height + rows * width + height * width),
+            transcendentals=0,
+        ),
+        name=name,
+    )(left, right)
+
 
 HEAD_DIM = 64
 
@@ -485,6 +987,164 @@
         hidden_bias_gradient,
     )
 
+def gather_weight(weight):
+    gathered = lax.all_gather(weight, ("clip", "frame"))
+    return gathered.reshape(8, 4 * weight.shape[0], weight.shape[1])
+
+
+def scatter_weight(blocks):
+    by_clip = lax.psum_scatter(blocks, "clip", scatter_dimension=0, tiled=False)
+    return lax.psum_scatter(by_clip, "frame", scatter_dimension=0, tiled=True).astype(F32)
+
+
+def exchange(values):
+    return lax.all_to_all(values, "frame", 0, 0, tiled=True)
+
+
+def to_groups(big, small):
+    big_part = big.reshape(4, 4, 4, 16, D).transpose(1, 2, 0, 3, 4)
+    small_part = small.reshape(4, 4, 1, 16, D).transpose(1, 2, 0, 3, 4)
+    return jnp.concatenate([big_part, small_part], axis=1)
+
+
+def from_groups(groups):
+    big = groups[:, :4].transpose(2, 0, 1, 3, 4).reshape(1, 4, 256, D)
+    small = groups[:, 4].transpose(1, 0, 2, 3).reshape(1, 4, 64, D)
+    return big, small
+
+
+def fast_body(
+    big_tokens,
+    small_tokens,
+    big_actions,
+    small_actions,
+    action_table,
+    norm_gain,
+    norm_bias,
+    spatial_inputs,
+    spatial_output,
+    temporal_inputs,
+    temporal_output,
+    up_weight,
+    down_weight,
+    branch_bias,
+    hidden_bias,
+    big_cotangent,
+    small_cotangent,
+):
+    packed = jnp.concatenate(
+        [
+            action_table.reshape(-1),
+            norm_gain.reshape(-1),
+            norm_bias.reshape(-1),
+            branch_bias.reshape(-1),
+            hidden_bias,
+        ]
+    )
+    smalls = lax.all_gather(packed, ("clip", "frame")).astype(F32)
+    rows17 = smalls[:, :544].reshape(32, 17, 32).transpose(1, 0, 2).reshape(17, D)
+    hidden_row = smalls[:, 544:].reshape(1, 4 * D)
+    table = rows17[0:8]
+    pad = jnp.zeros((5, D), F32)
+
+    def small_of(index):
+        return jnp.concatenate(
+            [
+                rows17[8 + index][None],
+                rows17[11 + index][None],
+                rows17[14 + index][None],
+                pad,
+            ]
+        )
+
+    smalls0, smalls1, smalls2 = small_of(0), small_of(1), small_of(2)
+    big_ids = jnp.repeat(big_actions.reshape(4, 1), 4, axis=1)
+    frame_ids = jnp.concatenate([big_ids, small_actions.reshape(1, 4)])
+    onehot = (frame_ids[..., None] == jnp.arange(8, dtype=jnp.int32)).astype(F32)
+    embed = jnp.sum(onehot[..., None] * table, axis=2)
+    tokens = jnp.concatenate(
+        [big_tokens.reshape(4, ROWS, D), small_tokens.reshape(1, ROWS, D)]
+    )
+    win_s = gather_weight(spatial_inputs)
+    wo_s = gather_weight(spatial_output)
+    win_t = gather_weight(temporal_inputs)
+    wo_t = gather_weight(temporal_output)
+    up = gather_weight(up_weight)
+    down = gather_weight(down_weight)
+    grads_out = to_groups(big_cotangent, small_cotangent)
+
+    x1, qkv_s, o_s, lse_s = attention_forward(True, tokens, embed, smalls0, win_s, wo_s)
+    x1p = exchange(x1).reshape(4, 5, 64, D)
+    dyp = exchange(grads_out).reshape(1280, D)
+    x2, qkv_t, o_t, lse_t = attention_forward(False, x1p, None, smalls1, win_t, wo_t)
+    x2f = x2.reshape(1280, D)
+    out, dx2, h3, act, du, sums2, hidden_sum = ffn(x2f, dyp, smalls2, hidden_row, up, down)
+    outputs = from_groups(exchange(out.reshape(4, 5, 4, 16, D)))
+    g_down = scatter_weight(outer(act, dyp, 8, 1024, "down_grad"))
+    g_up = scatter_weight(outer(h3, du, 8, 256, "up_grad"))
+    dx2g = dx2.reshape(4, 5, 64, D)
+    dx1, h2, dqkv_t, sums1 = attention_backward(
+        False, dx2g, x1p, None, smalls1, qkv_t, lse_t, win_t, wo_t
+    )
+    dx1f = exchange(dx1.reshape(4, 5, 4, 16, D))
+    dx2o = dx2g.transpose(1, 0, 2, 3).reshape(1280, D)
+    g_to = scatter_weight(outer(o_t.reshape(1280, D), dx2o, 8, 256, "temporal_out_grad"))
+    g_ti = scatter_weight(
+        outer(h2.reshape(1280, D), dqkv_t.reshape(1280, 3 * D), 8, 256, "temporal_in_grad")
+    )
+    big_grad, small_grad, frame_sums, h1, dqkv_s, dy1, sums0 = attention_backward(
+        True, dx1f, tokens, embed, smalls0, qkv_s, lse_s, win_s, wo_s
+    )
+    g_so = scatter_weight(
+        outer(o_s.reshape(1280, D), dy1.reshape(1280, D), 8, 256, "spatial_out_grad")
+    )
+    g_si = scatter_weight(
+        outer(h1.reshape(1280, D), dqkv_s.reshape(1280, 3 * D), 8, 256, "spatial_in_grad")
+    )
+    table_sum = jnp.sum(
+        onehot.reshape(20, 8)[:, :, None] * frame_sums.reshape(20, 1, D), axis=0
+    )
+    stacked = jnp.concatenate(
+        [
+            table_sum,
+            sums0[0:1],
+            sums1[0:1],
+            sums2[0:1],
+            sums0[1:2],
+            sums1[1:2],
+            sums2[1:2],
+            sums0[2:3],
+            sums1[2:3],
+            sums2[2:3],
+        ]
+    )
+    small_grads = jnp.concatenate(
+        [
+            stacked.reshape(17, 32, 32).transpose(1, 0, 2).reshape(32, 544),
+            hidden_sum.reshape(32, 128),
+        ],
+        axis=1,
+    )
+    mine = lax.psum_scatter(small_grads, ("clip", "frame"), scatter_dimension=0, tiled=False)
+    shard17 = mine[:544].reshape(17, 32)
+    return (
+        outputs[0],
+        outputs[1],
+        big_grad.reshape(1, 4, 256, D),
+        small_grad.reshape(1, 4, 64, D),
+        shard17[0:8],
+        shard17[8:11],
+        shard17[11:14],
+        g_si,
+        g_so,
+        g_ti,
+        g_to,
+        g_up,
+        g_down,
+        shard17[14:17],
+        mine[544:],
+    )
+
 
 def solution(mesh):
     placed = (
@@ -507,7 +1167,7 @@
         P("clip", "frame", None, None),
     )
     return jax.shard_map(
-        body,
+        fast_body if dict(mesh.shape) == {"clip": 8, "frame": 4} else body,
         mesh=mesh,
         in_specs=placed,
         out_specs=(

time: 1650 us -> 1350 us (0.82)
  matrix products: 441 us -> 0 us
  waiting for transfers between devices: 539 us -> 919 us
  Pallas kernels: 0 us -> 305 us
  local copies, waits for them, and re-layouts: 243 us -> 26.8 us
  blocking collectives: 231 us -> 42.4 us
  other arithmetic: 120 us -> 16.1 us
  starting transfers between devices: 47.2 us -> 16.8 us
    dot_general x62 -> x0, matrix products: 432 us -> none  [the longest x12 108 us: outer_sum(): lax.dot_general(flat_left, flat_right, (((0,), (0,)), ((), ())), preferre...]
    pallas_call x0 -> x11, Pallas kernels: none -> 305 us  [the longest x2 106 us: attention_backward(): pl.pallas_call(partial(bwd_kernel, spatial), grid=(5,), in_specs=in_specs...]
    all_gather x8 -> x6, waiting for transfers between devices: 0.05 us -> 295 us  [gather_weight(): gathered = lax.all_gather(weight, ('clip', 'frame'))]
    all_gather x14 -> x0, blocking collectives: 207 us -> none  [the longest x1 39.5 us: body(): lax.all_gather(hidden_bias, 'frame', axis=0, tiled=True)]
    reduce_scatter x7 -> x12, waiting for transfers between devices: 209 us -> 385 us  [the longest x6 247 us: scatter_weight(): by_clip = lax.psum_scatter(blocks, 'clip', scatter_dimension=0, tiled=False)]
    unnamed x41 -> x20, waiting for transfers between devices: 263 us -> 127 us
    reshape x17 -> x9, local copies, waits for them, and re-layouts: 77.8 us -> 5.28 us  [the longest x1 1.83 us: to_groups(): big_part = big.reshape(4, 4, 4, 16, D).transpose(1, 2, 0, 3, 4)]
    unnamed x327 -> x26, local copies, waits for them, and re-layouts: 74.9 us -> 3.91 us
  transfers between devices with their start and end apart: 36 -> 23, of which waited for: 19 -> 18; matrix products, arithmetic and copies ran while one was open for 37% -> 3% of each run, Pallas kernels for 0% -> 14%
where the time goes in v1:
time: 1350 us; the launch traced here: 1340 us
  waiting for transfers between devices  919 us (68%)
  Pallas kernels  305 us (23%)
  blocking collectives  42.4 us (3%)
  local copies, waits for them, and re-layouts  26.8 us (2%)
  starting transfers between devices  16.8 us (1%)
  other arithmetic  16.1 us (1%)
  between operations  14.6 us (1%)
    all_gather x6, waiting for transfers between devices, gather_weight(): gathered = lax.all_gather(weight, ('clip', 'frame'))  295 us
    reduce_scatter x6, waiting for transfers between devices, scatter_weight(): by_clip = lax.psum_scatter(blocks, 'clip', scatter_dimension=0, tiled=False)  247 us
    reduce_scatter x6, waiting for transfers between devices, scatter_weight(): lax.psum_scatter(by_clip, 'frame', scatter_dimension=0, tiled=True)  137 us
    unnamed x20, waiting for transfers between devices  127 us
    all_to_all x4, waiting for transfers between devices, exchange(): return lax.all_to_all(values, 'frame', 0, 0, tiled=True)  112 us
    pallas_call x2, Pallas kernels, attention_backward(): pl.pallas_call(partial(bwd_kernel, spatial), grid=(5,), in_specs=in_specs...  106 us
    pallas_call x6, Pallas kernels, outer(): pl.pallas_call(outer_kernel, grid=(height // tile,), in_specs=[pl.BlockSp...  74.9 us
    pallas_call x1, Pallas kernels, ffn(): pl.pallas_call(ffn_kernel, grid=(rows // ROWS,), in_specs=[tile, tile, pl...  65 us
  transfers between devices with their start and end apart: 23, of which 18 were waited for; matrix products, arithmetic and copies ran while one was open for 3% of the time, Pallas kernels for 14%

profile of v1, /device:TPU:0, one launch (start us, length us, event | category | flops | bytes accessed | tf_op | source)
XLA Modules:
  0.0 1340.1 jit_solution(6235832699700632944)
XLA Ops:
  15.2 42.4 %all-reduce = bf16[21504]{0:T(1024)(128)(2,1)S(1)} all-reduce(bf16[21504]{0:T(1024)(128)(2,1)S(1)} %dynamic-update-slice), channel_id=2, replica_groups=mesh['clip'=8,'frame'=4] {'clip','frame'}, use_global_device_ids=true, to_apply=%add | all-reduce | flops 21504 | bytes 86016
  60.4 1.7 pad_maximum_fusion.refs_0_.refs_1_
  62.8 7.3 all-gather.16.cloned.1.call-done
  70.1 71.0 %all-gather.14.cloned.1.call-done = bf16[8192,384]{1,0:T(8,128)(2,1)} async-done(((bf16[256,384]{1,0:T(8,128)(2,1)}), bf16[8192,384]{1,0:T(8,128)(2,1)}) %all-gather.14.cloned.1.call-update) | async-done | bytes 6291472 | tf_op jit(solution)/shard_map/all_gather | solution.py:991
  141.1 29.5 %spatial_fwd.1 = (bf16[4,5,4,16,1024]{4,3,2,1,0:T(8,128)(2,1)}, bf16[5,256,3072]{2,1,0:T(8,128)(2,1)}, bf16[5,256,1024]{2,1,0:T(8,128)(2,1)}, f32[5,256,128]{2,1,0:T(8,128)}) custom-call(bf16[5,256,1024]{2,1,0:T(8,128)(2,1)} %pad_maximum_fusion.refs_0_.refs_1_, f32[5,4,1024]{2,1,0:T(4,128)} %multiply_reduce_fusion.1.refs_1_.refs_2_, ...), custom_call_target="tpu_custom_call" | custom-call | flops 10737418240 | bytes 31457280 | tf_op jit(solution)/shard_map/spatial_fwd/pallas_call | solution.py:164
  170.7 3.7 all-to-all-start
  174.4 1.8 copy.66
  176.3 1.8 pad_maximum_fusion.1
  178.0 62.5 %all-to-all-done = bf16[4,5,4,16,1024]{4,3,2,1,0:T(8,128)(2,1)S(1)} async-done(((bf16[4,5,4,16,1024]{4,3,2,1,0:T(8,128)(2,1)}), bf16[4,5,4,16,1024]{4,3,2,1,0:T(8,128)(2,1)S(1)}, u32[]{:S(2)}, u32[]{:S(2)}) %all-to-all-start) | async-done | bytes 2621472 | tf_op jit(solution)/shard_map/all_to_all | solution.py:1001
  240.5 1.5 copy-done.1
  242.0 4.1 all-to-all-start.1
  246.8 88.2 %all-gather.18.cloned.1.call-done = bf16[8192,384]{1,0:T(8,128)(2,1)} async-done(((bf16[256,384]{1,0:T(8,128)(2,1)}), bf16[8192,384]{1,0:T(8,128)(2,1)}) %all-gather.18.cloned.1.call-update) | async-done | bytes 6291472 | tf_op jit(solution)/shard_map/all_gather | solution.py:991
  335.0 28.7 %temporal_fwd.1 = (bf16[4,5,64,1024]{3,2,1,0:T(8,128)(2,1)}, bf16[5,256,3072]{2,1,0:T(8,128)(2,1)}, bf16[5,256,1024]{2,1,0:T(8,128)(2,1)}, f32[5,256,128]{2,1,0:T(8,128)}) custom-call(bf16[4,5,64,1024]{3,2,1,0:T(8,128)(2,1)} %bitcast.59, f32[8,1024]{1,0:T(8,128)} %get-tuple-element.89.refs_1_.refs_2_, bf16[8,1024,384]{2,1,0:T(8,128)(2,1)} %bitcast.87, ...), custom_call_target="tpu_custom_call" | custom-call | flops 10737418240 | bytes 31457280 | tf_op jit(solution)/shard_map/temporal_fwd/pallas_call | solution.py:164
  363.8 49.7 %all-gather.22.cloned.1.call-done = bf16[8192,512]{1,0:T(8,128)(2,1)} async-done(((bf16[256,512]{1,0:T(8,128)(2,1)}), bf16[8192,512]{1,0:T(8,128)(2,1)}) %all-gather.22.cloned.1.call-update) | async-done | bytes 8388624 | tf_op jit(solution)/shard_map/all_gather | solution.py:991
  413.5 78.5 %all-gather.24.cloned.1.call-done = bf16[32768,128]{1,0:T(8,128)(2,1)} async-done(((bf16[1024,128]{1,0:T(8,128)(2,1)}), bf16[32768,128]{1,0:T(8,128)(2,1)}) %all-gather.24.cloned.1.call-update) | async-done | bytes 8388624 | tf_op jit(solution)/shard_map/all_gather | solution.py:991
  492.0 65.0 %ffn.1 = (bf16[1280,1024]{1,0:T(8,128)(2,1)}, bf16[1280,1024]{1,0:T(8,128)(2,1)}, bf16[1280,1024]{1,0:T(8,128)(2,1)}, bf16[1280,4096]{1,0:T(8,128)(2,1)}, bf16[1...) custom-call(bf16[1280,1024]{1,0:T(8,128)(2,1)} %bitcast.101, bf16[1280,1024]{1,0:T(8,128)(2,1)} %bitcast.57, ...), custom_call_target="tpu_custom_call" | custom-call | flops 42949672960 | bytes 52428800 | tf_op jit(solution)/shard_map/ffn/pallas_call | solution.py:432
  557.0 52.1 %temporal_bwd.1 = (bf16[4,5,64,1024]{3,2,1,0:T(8,128)(2,1)}, bf16[5,256,1024]{2,1,0:T(8,128)(2,1)}, bf16[5,256,3072]{2,1,0:T(8,128)(2,1)}, f32[8,1024]{1,0:T(8,128)}) custom-call(bf16[4,5,64,1024]{3,2,1,0:T(8,128)(2,1)} %bitcast.62, bf16[4,5,64,1024]{3,2,1,0:T(8,128)(2,1)} %bitcast.60, f32[8,1024]{1,0:T(8,128)} %get-tuple-element.89.refs_1_.refs_2_, ...), custom_call_target="tpu_custom_call" | custom-call | flops 10737418240 | bytes 41943040 | tf_op jit(solution)/shard_map/temporal_bwd/pallas_call | solution.py:351
  609.1 3.7 all-to-all-start.3
  612.9 3.6 copy.63
  616.4 6.7 temporal_out_grad.1
  623.2 49.7 %all-to-all-done.3.refs_0_ = bf16[4,5,4,16,1024]{4,3,2,1,0:T(8,128)(2,1)S(1)} async-done(((bf16[4,5,4,16,1024]{4,3,2,1,0:T(8,128)(2,1)}), bf16[4,5,4,16,1024]{4,3,2,1,0:T(8,128)(2,1)S(1)}, u32[]{:S(2)}, u32[]{:S(2)}) %all-to-all-start.3) | async-done | bytes 2621472 | tf_op jit(solution)/shard_map/all_to_all | solution.py:1001
  672.9 1.5 copy-done.2
  674.4 54.2 %spatial_bwd.1 = (f32[4,256,1024]{2,1,0:T(8,128)}, f32[256,1024]{1,0:T(8,128)}, f32[5,4,1024]{2,1,0:T(4,128)}, bf16[5,256,1024]{2,1,0:T(8,128)(2,1)}, bf16[5,256...) custom-call(bf16[4,5,4,16,1024]{4,3,2,1,0:T(8,128)(2,1)} %copy-done.2, ...), custom_call_target="tpu_custom_call" | custom-call | flops 10737418240 | bytes 41943040 | tf_op jit(solution)/shard_map/spatial_bwd/pallas_call | solution.py:351
  728.7 6.8 spatial_out_grad.1
  735.5 13.6 %temporal_in_grad.1 = bf16[8,1024,384]{2,1,0:T(8,128)(2,1)} custom-call(bf16[1280,1024]{1,0:T(8,128)(2,1)} %bitcast.98, bf16[1280,3072]{1,0:T(8,128)(2,1)} %bitcast.94), custom_call_target="tpu_custom_call" | custom-call | flops 8053063680 | bytes 16777216 | tf_op jit(solution)/shard_map/temporal_in_grad/pallas_call | solution.py:489
  749.2 17.5 %up_grad.1 = bf16[8,1024,512]{2,1,0:T(8,128)(2,1)} custom-call(bf16[1280,1024]{1,0:T(8,128)(2,1)} %get-tuple-element.64.left_ref, bf16[1280,4096]{1,0:T(8,128)(2,1)} %get-tuple-element.65.right_ref), custom_call_target="tpu_custom_call" | custom-call | flops 10737418240 | bytes 21495808 | tf_op jit(solution)/shard_map/up_grad/pallas_call | solution.py:489
  766.8 15.7 %down_grad.1 = bf16[8,4096,128]{2,1,0:T(8,128)(2,1)} custom-call(bf16[1280,4096]{1,0:T(8,128)(2,1)} %get-tuple-element.66.left_ref, bf16[1280,1024]{1,0:T(8,128)(2,1)} %bitcast.58), custom_call_target="tpu_custom_call" | custom-call | flops 10737418240 | bytes 21495808 | tf_op jit(solution)/shard_map/down_grad/pallas_call | solution.py:489
  782.6 14.5 %spatial_in_grad.1 = bf16[8,1024,384]{2,1,0:T(8,128)(2,1)} custom-call(bf16[1280,1024]{1,0:T(8,128)(2,1)} %bitcast.99, bf16[1280,3072]{1,0:T(8,128)(2,1)} %bitcast.95), custom_call_target="tpu_custom_call" | custom-call | flops 8053063680 | bytes 16777216 | tf_op jit(solution)/shard_map/spatial_in_grad/pallas_call | solution.py:489
  802.8 37.2 %reduce-scatter.21.cloned.1.call-done = bf16[1,1024,384]{2,1,0:T(8,128)(2,1)} async-done(((bf16[8,1024,384]{2,1,0:T(8,128)(2,1)}), bf16[1,1024,384]{2,1,0:T(8,128)(2,1)}) %reduce-scatter.21.cloned.1.call-update) | async-done | bytes 786448 | tf_op jit(solution)/shard_map/reduce_scatter | solution.py:996
  840.1 74.8 %reduce-scatter.29.cloned.1.call-done = bf16[1,1024,512]{2,1,0:T(8,128)(2,1)} async-done(((bf16[8,1024,512]{2,1,0:T(8,128)(2,1)}), bf16[1,1024,512]{2,1,0:T(8,128)(2,1)}) %reduce-scatter.29.cloned.1.call-update) | async-done | bytes 1048592 | tf_op jit(solution)/shard_map/reduce_scatter | solution.py:996
  914.9 4.6 all-to-all-start.2
  919.5 70.4 %reduce-scatter.33.cloned.1.call-done = bf16[1,4096,128]{2,1,0:T(8,128)(2,1)} async-done(((bf16[8,4096,128]{2,1,0:T(8,128)(2,1)}), bf16[1,4096,128]{2,1,0:T(8,128)(2,1)}) %reduce-scatter.33.cloned.1.call-update) | async-done | bytes 1048592 | tf_op jit(solution)/shard_map/reduce_scatter | solution.py:996
  990.0 64.9 %reduce-scatter.13.cloned.1.call-done = bf16[1,1024,384]{2,1,0:T(8,128)(2,1)} async-done(((bf16[8,1024,384]{2,1,0:T(8,128)(2,1)}), bf16[1,1024,384]{2,1,0:T(8,128)(2,1)}) %reduce-scatter.13.cloned.1.call-update) | async-done | bytes 786448 | tf_op jit(solution)/shard_map/reduce_scatter | solution.py:996
  1054.9 22.2 %reduce-scatter.27.cloned.1.call-done = bf16[256,128]{1,0:T(8,128)(2,1)} async-done(((bf16[1024,128]{1,0:T(8,128)(2,1)}), bf16[256,128]{1,0:T(8,128)(2,1)}) %reduce-scatter.27.cloned.1.call-update) | async-done | bytes 65552 | tf_op jit(solution)/shard_map/reduce_scatter | solution.py:997
  1077.2 1.5 convert_element_type.40
  1078.9 1.5 copy.60
  1081.2 122.8 %all-reduce.4.cloned.1.call-done = f32[32,672]{1,0:T(8,128)} async-done(((f32[32,672]{1,0:T(8,128)}), f32[32,672]{1,0:T(8,128)}) %all-reduce.4.cloned.1.call-update) | async-done | bytes 86032
  1208.3 1.3 dynamic-slice_bitcast_fusion
  1209.5 17.5 %reduce-scatter.19.cloned.1.call-done = bf16[256,128]{1,0:T(8,128)(2,1)} async-done(((bf16[1024,128]{1,0:T(8,128)(2,1)}), bf16[256,128]{1,0:T(8,128)(2,1)}) %reduce-scatter.19.cloned.1.call-update) | async-done | bytes 65552 | tf_op jit(solution)/shard_map/reduce_scatter | solution.py:997
  1227.1 1.5 convert_element_type.38
  1228.6 22.1 %reduce-scatter.23.cloned.1.call-done = bf16[256,384]{1,0:T(8,128)(2,1)} async-done(((bf16[1024,384]{1,0:T(8,128)(2,1)}), bf16[256,384]{1,0:T(8,128)(2,1)}) %reduce-scatter.23.cloned.1.call-update) | async-done | bytes 196624 | tf_op jit(solution)/shard_map/reduce_scatter | solution.py:997
  1250.6 1.7 convert_element_type.39
  1252.3 27.3 %reduce-scatter.31.cloned.1.call-done = bf16[256,512]{1,0:T(8,128)(2,1)} async-done(((bf16[1024,512]{1,0:T(8,128)(2,1)}), bf16[256,512]{1,0:T(8,128)(2,1)}) %reduce-scatter.31.cloned.1.call-update) | async-done | bytes 262160 | tf_op jit(solution)/shard_map/reduce_scatter | solution.py:997
  1279.6 1.8 convert_element_type.41
  1281.4 26.2 %reduce-scatter.35.cloned.1.call-done = bf16[1024,128]{1,0:T(8,128)(2,1)} async-done(((bf16[4096,128]{1,0:T(8,128)(2,1)}), bf16[1024,128]{1,0:T(8,128)(2,1)}) %reduce-scatter.35.cloned.1.call-update) | async-done | bytes 262160 | tf_op jit(solution)/shard_map/reduce_scatter | solution.py:997
  1307.6 1.8 convert_element_type.42
  1309.3 22.2 %reduce-scatter.15.cloned.1.call-done = bf16[256,384]{1,0:T(8,128)(2,1)} async-done(((bf16[1024,384]{1,0:T(8,128)(2,1)}), bf16[256,384]{1,0:T(8,128)(2,1)}) %reduce-scatter.15.cloned.1.call-update) | async-done | bytes 196624 | tf_op jit(solution)/shard_map/reduce_scatter | solution.py:997
  1331.6 1.7 convert_element_type.37
  (118 shorter events, 23.3 us)
Async XLA Ops:
  7.2 52.1 %copy-start.11 = (s32[1,4]{1,0:T(1,128)S(1)}, s32[1,4]{1,0:T(1,128)}, u32[]{:S(2)}) copy-start(s32[1,4]{1,0:T(1,128)} %param.19) | copy-start | bytes 52
  7.2 52.1 %copy-start.10 = (s32[1,4]{1,0:T(1,128)S(1)}, s32[1,4]{1,0:T(1,128)}, u32[]{:S(2)}) copy-start(s32[1,4]{1,0:T(1,128)} %param.20) | copy-start | bytes 52
  7.2 53.2 %copy-start.3 = (bf16[1,4,256,1024]{3,2,1,0:T(8,128)(2,1)S(1)}, bf16[1,4,256,1024]{3,2,1,0:T(8,128)(2,1)}, u32[]{:S(2)}) copy-start(bf16[1,4,256,1024]{3,2,1,0:T(8,128)(2,1)} %param.17) | copy-start | bytes 6291460
  7.2 53.1 %copy-start.4 = (bf16[1,4,64,1024]{3,2,1,0:T(8,128)(2,1)S(1)}, bf16[1,4,64,1024]{3,2,1,0:T(8,128)(2,1)}, u32[]{:S(2)}) copy-start(bf16[1,4,64,1024]{3,2,1,0:T(8,128)(2,1)} %param.18) | copy-start | bytes 1572868
  7.2 62.9 %all-gather.16.cloned.1.call-start = ((), (), s32[]{:S(2)}) async-start(), calls=%async_computation.29 | async-start | bytes 2162688 | tf_op jit(solution)/shard_map/all_gather | solution.py:991
  8.0 133.2 %all-gather.14.cloned.1.call-start = ((), (), s32[]{:S(2)}) async-start(), calls=%async_computation.28 | async-start | bytes 6488064 | tf_op jit(solution)/shard_map/all_gather | solution.py:991
  8.7 238.1 %all-gather.20.cloned.1.call-start = ((), (), s32[]{:S(2)}) async-start(), calls=%async_computation.31 | async-start | bytes 2162688 | tf_op jit(solution)/shard_map/all_gather | solution.py:991
  9.4 325.6 %all-gather.18.cloned.1.call-start = ((), (), s32[]{:S(2)}) async-start(), calls=%async_computation.30 | async-start | bytes 6488064 | tf_op jit(solution)/shard_map/all_gather | solution.py:991
  10.0 403.5 %all-gather.22.cloned.1.call-start = ((), (), s32[]{:S(2)}) async-start(), calls=%async_computation.32 | async-start | bytes 8650752 | tf_op jit(solution)/shard_map/all_gather | solution.py:991
  10.6 481.4 %all-gather.24.cloned.1.call-start = ((), (), s32[]{:S(2)}) async-start(), calls=%async_computation.33 | async-start | bytes 8650752 | tf_op jit(solution)/shard_map/all_gather | solution.py:991
  59.4 2.7 copy-start.7
  170.7 69.8 %all-to-all-start = ((bf16[4,5,4,16,1024]{4,3,2,1,0:T(8,128)(2,1)}), bf16[4,5,4,16,1024]{4,3,2,1,0:T(8,128)(2,1)S(1)}, u32[]{:S(2)}, u32[]{:S(2)}) async-start(bf16[4,5,4,16,1024]{4,3,2,1,0:T(8,128)(2,1)} %get-tuple-element.41), calls=%async_computation | async-start | bytes 5242880 | tf_op jit(solution)/shard_map/all_to_all | solution.py:1001
  174.4 1.9 copy-start.5
  240.5 1.5 copy-start.1
  242.0 121.7 %all-to-all-start.1 = ((bf16[4,5,4,16,1024]{4,3,2,1,0:T(8,128)(2,1)}), bf16[4,5,4,16,1024]{4,3,2,1,0:T(8,128)(2,1)S(1)}, u32[]{:S(2)}, u32[]{:S(2)}) async-start(bf16[4,5,4,16,1024]{4,3,2,1,0:T(8,128)(2,1)} %pad_maximum_fusion.1), calls=%async_computation.1 | async-start | bytes 5242880 | tf_op jit(solution)/shard_map/all_to_all | solution.py:1001
  363.8 128.2 %copy-start = (bf16[4,5,4,16,1024]{4,3,2,1,0:T(8,128)(2,1)}, bf16[4,5,4,16,1024]{4,3,2,1,0:T(8,128)(2,1)S(1)}, u32[]{:S(2)}) copy-start(bf16[4,5,4,16,1024]{4,3,2,1,0:T(8,128)(2,1)S(1)} %all-to-all-done.1) | copy-start | bytes 7864324
  609.1 63.8 %all-to-all-start.3 = ((bf16[4,5,4,16,1024]{4,3,2,1,0:T(8,128)(2,1)}), bf16[4,5,4,16,1024]{4,3,2,1,0:T(8,128)(2,1)S(1)}, u32[]{:S(2)}, u32[]{:S(2)}) async-start(bf16[4,5,4,16,1024]{4,3,2,1,0:T(8,128)(2,1)} %bitcast.61), calls=%async_computation.3 | async-start | bytes 5242880 | tf_op jit(solution)/shard_map/all_to_all | solution.py:1001
  612.8 186.1 %reduce-scatter.25.cloned.1.call-start = ((), (), s32[]{:S(2)}) async-start(), calls=%async_computation.22 | async-start | bytes 2359296 | tf_op jit(solution)/shard_map/reduce_scatter | solution.py:996
  623.2 179.1 %reduce-scatter.17.cloned.1.call-start = ((), (), s32[]{:S(2)}) async-start(), calls=%async_computation.18 | async-start | bytes 2359296 | tf_op jit(solution)/shard_map/reduce_scatter | solution.py:996
  672.9 1.5 copy-start.2
  735.5 104.6 %reduce-scatter.21.cloned.1.call-start = ((), (), s32[]{:S(2)}) async-start(), calls=%async_computation.20 | async-start | bytes 7077888 | tf_op jit(solution)/shard_map/reduce_scatter | solution.py:996
  749.2 165.7 %reduce-scatter.29.cloned.1.call-start = ((), (), s32[]{:S(2)}) async-start(), calls=%async_computation.24 | async-start | bytes 9437184 | tf_op jit(solution)/shard_map/reduce_scatter | solution.py:996
  766.8 223.1 %reduce-scatter.33.cloned.1.call-start = ((), (), s32[]{:S(2)}) async-start(), calls=%async_computation.26 | async-start | bytes 9437184 | tf_op jit(solution)/shard_map/reduce_scatter | solution.py:996
  782.6 272.3 %reduce-scatter.13.cloned.1.call-start = ((), (), s32[]{:S(2)}) async-start(), calls=%async_computation.16 | async-start | bytes 7077888 | tf_op jit(solution)/shard_map/reduce_scatter | solution.py:996
  797.2 0.7 copy-start.8
  797.2 2.7 copy-start.6
  797.2 4.3 copy-start.9
  797.2 280.0 %reduce-scatter.27.cloned.1.call-start = ((), (), s32[]{:S(2)}) async-start(), calls=%async_computation.23 | async-start | bytes 327680 | tf_op jit(solution)/shard_map/reduce_scatter | solution.py:997
  799.0 405.0 %all-reduce.4.cloned.1.call-start = ((), (), s32[]{:S(2)}) async-start(), calls=%async_computation.34 | async-start | bytes 196608
  802.2 424.9 %reduce-scatter.19.cloned.1.call-start = ((), (), s32[]{:S(2)}) async-start(), calls=%async_computation.19 | async-start | bytes 327680 | tf_op jit(solution)/shard_map/reduce_scatter | solution.py:997
  802.8 447.8 %reduce-scatter.23.cloned.1.call-start = ((), (), s32[]{:S(2)}) async-start(), calls=%async_computation.21 | async-start | bytes 983040 | tf_op jit(solution)/shard_map/reduce_scatter | solution.py:997
  840.0 439.5 %reduce-scatter.31.cloned.1.call-start = ((), (), s32[]{:S(2)}) async-start(), calls=%async_computation.25 | async-start | bytes 1310720 | tf_op jit(solution)/shard_map/reduce_scatter | solution.py:997
  914.9 163.8 %all-to-all-start.2 = ((bf16[4,5,4,16,1024]{4,3,2,1,0:T(8,128)(2,1)}), bf16[4,5,4,16,1024]{4,3,2,1,0:T(8,128)(2,1)S(1)}, u32[]{:S(2)}, u32[]{:S(2)}) async-start(bf16[4,5,4,16,1024]{4,3,2,1,0:T(8,128)(2,1)} %bitcast.56), calls=%async_computation.2 | async-start | bytes 5242880 | tf_op jit(solution)/shard_map/all_to_all | solution.py:1001
  919.5 388.0 %reduce-scatter.35.cloned.1.call-start = ((), (), s32[]{:S(2)}) async-start(), calls=%async_computation.27 | async-start | bytes 1310720 | tf_op jit(solution)/shard_map/reduce_scatter | solution.py:997
  989.9 341.6 %reduce-scatter.15.cloned.1.call-start = ((), (), s32[]{:S(2)}) async-start(), calls=%async_computation.17 | async-start | bytes 983040 | tf_op jit(solution)/shard_map/reduce_scatter | solution.py:997
Sparse Core Ops, SparseCore 0:
  11.0 59.1 all-gather.15
  73.0 68.1 all-gather.13
  144.1 83.8 all-gather.19
  230.7 104.3 all-gather.17
  337.8 75.6 all-gather.21
  416.3 75.6 all-gather.23
  623.3 41.5 reduce-scatter.24
  735.6 39.2 reduce-scatter.16
  778.3 61.7 reduce-scatter.20
  843.3 71.5 reduce-scatter.28
  918.4 71.5 reduce-scatter.32
  993.1 61.7 reduce-scatter.12
  1057.2 19.9 reduce-scatter.26
  1083.2 120.7 all-reduce.3
  1206.1 20.9 reduce-scatter.18
  1229.2 21.3 reduce-scatter.22
  1252.8 26.7 reduce-scatter.30
  1281.7 25.7 reduce-scatter.34
  1309.9 21.6 reduce-scatter.14
